TPU v7x, 256 devices: a whole 4x4x8 slice. The times are simulated.
256 devices in a mesh: frame: 4 (over x), space: 64 (over z, y, core).
Axes of the slice: x: 4, y: 4, z: 8, core: 2. Of those that a mesh axis runs over, the one named last changes fastest.
Arguments:
- queries: bfloat16 [32768, 3072], P(('frame', 'space')), as said below
- keys: bfloat16 [32768, 3072], P(('frame', 'space')), as said below
- values: bfloat16 [32768, 3072], P(('frame', 'space')), may hold values from -5 to 5
- level_weight: float32 [3, 24, 32768], P(None, None, ('frame', 'space')), may hold values from 0.2 to 2
- frame_len: int32 [256, 4], P(('frame', 'space')), may hold values from 1 to 53, 128 in all within a row
- window_back: int32 [256, 4], P(('frame', 'space')), may hold values from 2 to 63
Outputs:
- mixed: bfloat16 [32768, 3072], P(('frame', 'space'))
Inputs may be any that keep to these rules, and one draw needn't show every extreme that they name: `queries`: entries up to 60 in magnitude. `keys`: entries up to 4 in magnitude. `frame_len`: each row is the frame lengths of one device's 128 tokens, summing to 128; the longest frame of each row has exactly 53 tokens.
All inputs are finite; a program needn't handle non-finite values.
Results may differ from a plain program's by a relative error of at most 0.0085.
Values may be sent and summed in bfloat16 or wider, within the bound.
A program may use at most 64 MiB of HBM per device.

v0:
```python
import math

import jax
import jax.numpy as jnp
from jax import lax
from jax.sharding import PartitionSpec as P

HEADS = 24
HEAD_DIM = 128


EPSILON = 1e-06


def unit_rows(matrix):
    return (matrix * lax.rsqrt(jnp.mean(matrix * matrix, -1, keepdims=True) + EPSILON)).astype(
        jnp.bfloat16
    )


def visible_mask(lengths, backward, count):
    starts = jnp.cumsum(lengths) - lengths
    lowest = jnp.maximum(starts - backward, 0)
    position = jnp.arange(count, dtype=jnp.int32)
    inside = (position[:, None] >= starts[None, :]).astype(jnp.int32)
    frame_of = jnp.sum(inside, 1) - 1
    onehot = frame_of[:, None] == jnp.arange(lengths.shape[0], dtype=jnp.int32)[None, :]
    floor_row = jnp.sum(jnp.where(onehot, lowest[None, :], 0), 1)
    return (position[None, :] <= position[:, None]) & (position[None, :] >= floor_row[:, None])


def causal_mix(query_heads, key_heads, value_heads, visible, heads, head_dim):
    pieces = []
    for first_head in range(0, heads, 4):
        query_part = query_heads[:, first_head : first_head + 4]
        key_part = key_heads[:, first_head : first_head + 4]
        value_part = value_heads[:, first_head : first_head + 4]
        scores = jnp.einsum(
            "thd,shd->hts", query_part, key_part, preferred_element_type=jnp.float32
        ) / math.sqrt(head_dim)
        scores = jnp.where(visible[None], scores, -jnp.inf)
        row_max = jnp.max(scores, -1, keepdims=True)
        weights = jnp.exp(scores - row_max)
        totals = jnp.sum(weights, -1)
        mixed_part = jnp.einsum(
            "hts,shd->thd",
            weights.astype(jnp.bfloat16),
            value_part,
            preferred_element_type=jnp.float32,
        )
        pieces.append(mixed_part / jnp.transpose(totals)[:, :, None])
    return jnp.concatenate(pieces, 1)


def body(queries, keys, values, level_weight, frame_len, window_back):
    tok_rows = queries.shape[0]
    frames_total = lax.axis_size("frame")
    frame_pos = lax.axis_index("frame")
    space_count = lax.axis_size("space")
    query_heads = queries.reshape(tok_rows, HEADS, HEAD_DIM)
    key_heads = keys.reshape(tok_rows, HEADS, HEAD_DIM)
    value_heads = values.reshape(tok_rows, HEADS, HEAD_DIM)
    normal_k = unit_rows(key_heads.astype(jnp.float32))
    local_state = jnp.einsum(
        "thd,the->hde", normal_k, value_heads, preferred_element_type=jnp.float32
    )
    state_rows = local_state.reshape(HEADS * HEAD_DIM, HEAD_DIM)
    block_part = lax.psum(state_rows, "space")
    tree_depth = frames_total.bit_length() - 1
    levels = []
    all_blocks = lax.all_gather(
        block_part[None].astype(jnp.bfloat16), "frame", axis=0, tiled=True
    ).astype(jnp.float32)
    block_ids = jnp.arange(frames_total, dtype=jnp.int32)
    for bit_index in range(tree_depth):
        start_block = frame_pos // 2 ** (bit_index + 1) * 2 ** (bit_index + 1)
        bit_set = frame_pos // 2**bit_index % 2
        inside = (
            (block_ids >= start_block) & (block_ids < start_block + 2**bit_index) & (bit_set == 1)
        )
        levels.append(jnp.sum(jnp.where(inside[:, None, None], all_blocks, 0.0), 0))
    level_rows = jnp.stack(levels).astype(jnp.bfloat16)
    level_heads = level_rows.reshape(tree_depth, HEADS, HEAD_DIM, HEAD_DIM)
    visible = visible_mask(frame_len[0], window_back[0], tok_rows)
    local_mix = causal_mix(query_heads, key_heads, value_heads, visible, HEADS, HEAD_DIM)
    result = local_mix * jnp.transpose(level_weight[0])[:, :, None]
    normal_q = unit_rows(query_heads.astype(jnp.float32))
    level_reads = jnp.einsum(
        "thd,lhde->lthe", normal_q, level_heads, preferred_element_type=jnp.float32
    )
    block_tokens = tok_rows * space_count
    for level_index in range(tree_depth):
        level_scale = 1.0 / math.sqrt(HEAD_DIM * 2**level_index * block_tokens)
        result = result + jnp.transpose(level_weight[1 + level_index])[:, :, None] * (
            level_scale * level_reads[level_index]
        )
    return result.reshape(tok_rows, HEADS * HEAD_DIM).astype(jnp.bfloat16)


def solution(mesh):
    return jax.shard_map(
        body,
        mesh=mesh,
        in_specs=(
            P(("frame", "space"), None),
            P(("frame", "space"), None),
            P(("frame", "space"), None),
            P(None, None, ("frame", "space")),
            P(("frame", "space"), None),
            P(("frame", "space"), None),
        ),
        out_specs=P(("frame", "space"), None),
        check_vma=False,
    )
```

profile of v0, /device:TPU:7, one launch (start us, length us, event | category | flops | bytes accessed | tf_op | source)
XLA Modules:
  0.0 330.5 jit_solution(7249709284273984305)
XLA Ops:
  6.5 1.6 copy.53
  8.1 0.4 copy.55
  8.7 0.7 fusion.32
  9.4 264.1 %all-reduce.1 = bf16[3072,128]{1,0:T(8,128)(2,1)} all-reduce(f32[3072,128]{1,0:T(8,128)S(1)} %bitcast.114), channel_id=1, replica_groups=mesh['frame'=4,'space'=64] {'space'}, use_global_device_ids=true, to_apply=%region_16.17 | all-reduce | flops 393216 | bytes 2359296 | tf_op jit(solution)/shard_map/psum | solution.py:68
  274.0 1.2 copy.51
  275.2 1.2 fusion.75
  276.5 1.2 fusion.76
  277.8 1.2 fusion.77
  279.1 1.2 fusion.78
  280.4 1.2 fusion.79
  281.6 1.2 fusion.80
  284.2 1.6 copy.78
  286.3 27.1 %all-gather.3.cloned.1.call-done = bf16[12288,128]{1,0:T(8,128)(2,1)} async-done(((bf16[3072,128]{1,0:T(8,128)(2,1)}), bf16[12288,128]{1,0:T(8,128)(2,1)}) %all-gather.3.cloned.1.call-update) | async-done | bytes 3145744 | tf_op jit(solution)/shard_map/all_gather | solution.py:71
  313.3 3.1 fusion
  316.5 0.4 copy.73
  316.8 0.4 copy.74
  317.2 0.6 convolution_bitcast_fusion
  318.0 1.6 copy.77
  319.6 0.5 copy.80
  320.1 0.5 mul.97
  320.6 0.5 mul.104
  321.1 0.4 copy-done.2
  321.5 0.5 copy-done.3
  322.0 1.6 fusion.7
  (46 shorter events, 2.8 us)
Async XLA Ops:
  6.5 1.6 copy-start.4
  6.5 306.8 %all-gather.3.cloned.1.call-start = ((), (), s32[]{:S(2)}) async-start(), calls=%async_computation | async-start | bytes 3932160 | tf_op jit(solution)/shard_map/all_gather | solution.py:71
  8.1 1.3 copy-start.1
  9.4 264.2 %copy-start.7 = (s32[1,4]{1,0:T(1,128)S(1)}, s32[1,4]{1,0:T(1,128)}, u32[]{:S(2)}) copy-start(s32[1,4]{1,0:T(1,128)} %param.10) | copy-start | bytes 52
  9.4 264.4 %copy-start.8 = (s32[1,4]{1,0:T(1,128)S(1)}, s32[1,4]{1,0:T(1,128)}, u32[]{:S(2)}) copy-start(s32[1,4]{1,0:T(1,128)} %param.11) | copy-start | bytes 52
  9.4 264.6 %copy-start.5 = (bf16[128,3072]{1,0:T(8,128)(2,1)S(1)}, bf16[128,3072]{1,0:T(8,128)(2,1)}, u32[]{:S(2)}) copy-start(bf16[128,3072]{1,0:T(8,128)(2,1)} %param.6) | copy-start | bytes 2359300
  279.0 3.9 %copy-start.6 = (f32[3,24,128]{2,1,0:T(8,128)S(1)}, f32[3,24,128]{2,1,0:T(8,128)}, u32[]{:S(2)}) copy-start(f32[3,24,128]{2,1,0:T(8,128)} %param.9) | copy-start | bytes 110596
  284.2 1.8 copy-start
  320.1 1.4 copy-start.2
  320.1 1.9 copy-start.3
Sparse Core Ops, SparseCore 0:
  273.7 39.5 all-gather.2
where the time goes:
time: 333 us; the launch traced here: 330 us
  blocking collectives  264 us (79%)
  waiting for transfers between devices  27.1 us (8%)
  between operations  13.7 us (4%)
  local copies, waits for them, and re-layouts  9.88 us (3%)
  matrix products  9.67 us (3%)
  other arithmetic  6 us (2%)
    psum x1, blocking collectives, body(): block_part = lax.psum(state_rows, 'space')  264 us
    all_gather x1, waiting for transfers between devices, body(): lax.all_gather(block_part[None].astype(jnp.bfloat16), 'frame', axis=0, ti...  27.1 us
    dot_general x6, matrix products, causal_mix(): jnp.einsum('thd,shd->hts', query_part, key_part, preferred_element_type=j...  7.32 us
  transfers between devices with their start and end apart: 1, of which 1 were waited for; matrix products, arithmetic and copies ran while one was open for 4% of the time, Pallas kernels for 0%

commit v1 on v0

v1 whole, which is shorter than its diff:
```python
import functools
import math

import jax
import jax.numpy as jnp
from jax import lax
from jax.experimental import pallas as pl
from jax.experimental.pallas import tpu as pltpu
from jax.sharding import PartitionSpec as P

MESH = pl.DeviceIdType.MESH
HEADS = 24
HALF = 12
D = 128
EPS = 1e-06
NY = 4
NZ = 8
CH = 3
CR = CH * D
HR = CR // 2
PR = CR // NZ
ORDER = (0, 1, 7, 2, 6, 3, 5, 4)
GO_RIGHT = (0, 7, 2, 5)


def kernel(
    block_tokens,
    flen,
    wback,
    lw,
    q_hbm,
    k_hbm,
    v_hbm,
    out_hbm,
    q,
    k,
    v,
    bias,
    wrows,
    wt,
    loc,
    qs,
    part,
    sib_out,
    sib_in,
    y_out,
    y_opp,
    y_in,
    z_out,
    z_in,
    x_out,
    x_in,
    lev,
    out,
    load_sem,
    sib_s,
    sib_r,
    y_s,
    y_r,
    z_s,
    z_r,
    x_s,
    x_r,
    gz_s,
    gz_r,
    gy_s,
    gy_r,
    gr_s,
    gr_r,
    gs_s,
    gs_r,
    out_sem,
):
    f = lax.axis_index("frame")
    s = lax.axis_index("space")
    c = lax.rem(s, 2)
    y = lax.rem(s // 2, NY)
    z = s // (2 * NY)
    right = lax.rem(y + 1, NY)
    left = lax.rem(y + NY - 1, NY)
    opp = lax.rem(y + 2, NY)

    def at(zz, yy, cc):
        return (zz * NY + yy) * 2 + cc

    sib = (f, at(z, y, 1 - c))
    to_right = (f, at(z, right, c))
    to_left = (f, at(z, left, c))

    def z_peer(step):
        return (f, at(lax.rem(z + step, NZ), y, c))

    def cols(head, count=1):
        return pl.ds(pl.multiple_of(head * D, D), count * D)

    def send(src, dst, ssem, rsem, dev):
        return pltpu.make_async_remote_copy(
            src_ref=src, dst_ref=dst, send_sem=ssem, recv_sem=rsem, device_id=dev, device_id_type=MESH
        )

    other = cols((1 - c) * HALF, HALF)
    mine = cols(c * HALF, HALF)
    loads = []
    for i, (src, dst, cc) in enumerate(
        ((k_hbm, k, other), (v_hbm, v, other), (k_hbm, k, mine), (v_hbm, v, mine))
    ):
        cp = pltpu.make_async_copy(src.at[:, cc], dst.at[:, cc], load_sem.at[i])
        cp.start()
        loads.append(cp)
    q_load = pltpu.make_async_copy(q_hbm, q, load_sem.at[4])
    q_load.start()

    barrier = pltpu.get_barrier_semaphore()
    peers = [sib, to_right, to_left]
    peers += [z_peer(i) for i in range(1, NZ)]
    peers += [(lax.rem(f + i, 4), s) for i in range(1, 4)]
    for dev in peers:
        pl.semaphore_signal(barrier, inc=1, device_id=dev, device_id_type=MESH)

    row = lax.broadcasted_iota(jnp.int32, (D, D), 0)
    col = lax.broadcasted_iota(jnp.int32, (D, D), 1)
    floor = jnp.full((D, D), 0, jnp.int32)
    start = 0
    for i in range(4):
        low = jnp.maximum(start - wback[0, i], 0)
        floor = jnp.where(row >= start, low, floor)
        start = start + flen[0, i]
    bias[...] = jnp.where((col <= row) & (col >= floor), 0.0, -jnp.inf)
    scale1 = 1.0 / math.sqrt(D * block_tokens)
    scale2 = 1.0 / math.sqrt(D * 2 * block_tokens)
    wrows[...] = jnp.zeros_like(wrows)
    wrows[0:HEADS] = lw[0]
    wrows[HEADS : 2 * HEADS] = jnp.where(f == 2, lw[2] * scale2, lw[1] * scale1)
    wrows[2 * HEADS : 3 * HEADS] = lw[2] * scale2
    wt[...] = jnp.transpose(wrows[...])

    def weight(index):
        return jnp.sum(jnp.where(col == index, wt[...], 0.0), -1, keepdims=True)

    def state(head):
        kk = k[:, cols(head)].astype(jnp.float32)
        kn = (kk * lax.rsqrt(jnp.mean(kk * kk, -1, keepdims=True) + EPS)).astype(jnp.bfloat16)
        return lax.dot_general(
            kn, v[:, cols(head)], (((0,), (0,)), ((), ())), preferred_element_type=jnp.float32
        )

    def attend(first, last):
        @pl.loop(first, last)
        def _(j):
            for i in range(CH):
                h = j * CH + i
                qq = q[:, cols(h)]
                scores = lax.dot_general(
                    qq, k[:, cols(h)], (((1,), (1,)), ((), ())), preferred_element_type=jnp.float32
                )
                scores = scores + bias[...]
                top = jnp.max(scores, -1, keepdims=True)
                p = jnp.exp((scores - top) * (1.0 / math.sqrt(D)))
                total = jnp.sum(p, -1, keepdims=True)
                mix = jnp.dot(p.astype(jnp.bfloat16), v[:, cols(h)], preferred_element_type=jnp.float32)
                loc[:, cols(h)] = mix * (weight(h) / total)
                q32 = qq.astype(jnp.float32)
                r = lax.rsqrt(jnp.mean(q32 * q32, -1, keepdims=True) + EPS)
                qs[0, :, cols(h)] = (q32 * (r * weight(HEADS + h))).astype(jnp.bfloat16)
                qs[1, :, cols(h)] = (q32 * (r * weight(2 * HEADS + h))).astype(jnp.bfloat16)

    def rows(chunk, first=0, count=CR):
        return pl.ds(pl.multiple_of(chunk * CR + first, PR), count)

    def sib_copy(j, yc):
        return send(sib_out.at[rows(yc)], sib_in.at[rows(yc)], sib_s.at[j], sib_r.at[j], sib)

    def chunk_at(j):
        return lax.rem(y + 2 - j + NY, NY)

    loads[0].wait()
    loads[1].wait()

    pl.semaphore_wait(barrier, len(peers))

    y_copies = [
        send(y_out.at[0], y_opp.at[0], y_s.at[0], y_r.at[0], to_right),
        send(y_out.at[1], y_opp.at[1], y_s.at[1], y_r.at[1], to_left),
        send(y_out.at[2], y_in.at[0, pl.ds(HR, HR)], y_s.at[2], y_r.at[2], to_right),
        send(y_out.at[3], y_in.at[1, pl.ds(0, HR)], y_s.at[3], y_r.at[3], to_left),
        send(y_out.at[4], y_in.at[0, pl.ds(0, HR)], y_s.at[4], y_r.at[4], to_right),
        send(y_out.at[5], y_in.at[1, pl.ds(HR, HR)], y_s.at[5], y_r.at[5], to_left),
    ]

    def z_copy(step):
        dst_z = lax.rem(z + step, NZ)
        return send(
            z_out.at[pl.ds(pl.multiple_of(dst_z * PR, PR), PR)],
            z_in.at[step],
            z_s.at[step],
            z_r.at[step],
            z_peer(step),
        )

    def x_copy(src_f, dst_f):
        return send(x_out, x_in.at[src_f], x_s.at[dst_f], x_r.at[src_f], (dst_f, s))

    sending = f < 3

    @pl.when(sending)
    def _():
        @pl.loop(0, NY)
        def _(j):
            yc = chunk_at(j)
            for i in range(CH):
                sib_out[pl.ds(pl.multiple_of(yc * CR + i * D, D), D)] = state(
                    (1 - c) * HALF + yc * CH + i
                ).astype(jnp.bfloat16)
            sib_copy(j, yc).start()

    loads[2].wait()
    loads[3].wait()

    @pl.when(sending)
    def _():
        @pl.loop(0, NY)
        def _(j):
            yc = chunk_at(j)
            for i in range(CH):
                part[pl.ds(pl.multiple_of(yc * CR + i * D, D), D)] = state(c * HALF + yc * CH + i)

        def add_sib(j):
            yc = chunk_at(j)
            sib_copy(j, yc).wait_recv()
            return part[rows(yc)] + sib_in[rows(yc)].astype(jnp.float32)

        total = add_sib(0).astype(jnp.bfloat16)
        y_out[0] = total[:HR]
        y_out[1] = total[HR:]
        y_copies[0].start()
        y_copies[1].start()
        total = add_sib(1)
        part[rows(right)] = total
        y_out[2] = total[HR:].astype(jnp.bfloat16)
        y_copies[2].start()
        total = add_sib(3)
        part[rows(left)] = total
        y_out[3] = total[:HR].astype(jnp.bfloat16)
        y_copies[3].start()
        part[rows(y)] = add_sib(2)

    q_load.wait()
    attend(0, 3)

    @pl.when(sending)
    def _():
        y_copies[0].wait_recv()
        y_out[4] = (part[rows(right, 0, HR)] + y_opp[0].astype(jnp.float32)).astype(jnp.bfloat16)
        y_copies[4].start()
        y_copies[1].wait_recv()
        y_out[5] = (part[rows(left, HR, HR)] + y_opp[1].astype(jnp.float32)).astype(jnp.bfloat16)
        y_copies[5].start()

    attend(3, 5)

    @pl.when(sending)
    def _():
        for i in range(2, 6):
            y_copies[i].wait_recv()
        total = part[rows(y)] + y_in[0].astype(jnp.float32) + y_in[1].astype(jnp.float32)
        part[rows(y)] = total
        z_out[...] = total.astype(jnp.bfloat16)
        for i in (4, 3, 5, 2, 6, 1, 7):
            z_copy(i).start()

    attend(5, 7)

    own_rows = pl.ds(pl.multiple_of(z * PR, PR), PR)

    @pl.when(sending)
    def _():
        total = part[pl.ds(pl.multiple_of(y * CR + z * PR, PR), PR)]
        for i in range(1, NZ):
            z_copy(i).wait_recv()
            total = total + z_in[i].astype(jnp.float32)
        x_out[...] = total.astype(jnp.bfloat16)

        for src in range(3):

            @pl.when(f == src)
            def _():
                for dst in range(3, src, -1):
                    x_copy(src, dst).start()

    attend(7, 8)

    chunk = c * NY + y
    piece = pl.ds(pl.multiple_of(chunk * CR + z * PR, PR), PR)

    @pl.when(f == 1)
    def _():
        x_copy(0, 1).wait_recv()
        lev[0, piece] = x_in[0]

    @pl.when(f == 2)
    def _():
        x_copy(0, 2).wait_recv()
        x_copy(1, 2).wait_recv()
        lev[0, piece] = (x_in[0].astype(jnp.float32) + x_in[1].astype(jnp.float32)).astype(jnp.bfloat16)

    @pl.when(f == 3)
    def _():
        for src in range(3):
            x_copy(src, 3).wait_recv()
        lev[0, piece] = x_in[2]
        lev[1, piece] = (x_in[0].astype(jnp.float32) + x_in[1].astype(jnp.float32)).astype(jnp.bfloat16)

    def put(head):
        cp = pltpu.make_async_copy(out.at[:, cols(head, CH)], out_hbm.at[:, cols(head, CH)], out_sem.at[head // CH])
        cp.start()

    def gather(n):
        def block(yc, step):
            zz = lax.rem(z + NZ - step, NZ)
            at_row = pl.multiple_of((c * NY + yc) * CR + zz * PR, PR)
            return lev.at[pl.ds(0, n), pl.ds(at_row, PR)]

        def gz(step):
            return send(block(y, 0), block(y, 0), gz_s.at[step], gz_r.at[step], z_peer(step))

        def gy(side, step):
            dev = to_right if side == 0 else to_left
            return send(block(y, step), block(y, step), gy_s.at[side, step], gy_r.at[side, step], dev)

        def relay(step):
            if step in GO_RIGHT:
                return send(block(left, step), block(left, step), gr_s.at[step], gr_r.at[step], to_right)
            return send(block(right, step), block(right, step), gr_s.at[step], gr_r.at[step], to_left)

        def whole(yc, cc):
            return lev.at[pl.ds(0, n), pl.ds(pl.multiple_of((cc * NY + yc) * CR, CR), CR)]

        def share(j, yc):
            return send(whole(yc, c), whole(yc, c), gs_s.at[j], gs_r.at[j], sib)

        def share_piece(step):
            return send(block(opp, step), block(opp, step), gs_s.at[3 + step], gs_r.at[3 + step], sib)

        def read(chunk_index):
            for i in range(CH):
                h = chunk_index * CH + i
                value = loc[:, cols(h)]
                for m in range(n):
                    value = value + jnp.dot(
                        qs[m, :, cols(h)], lev[m, pl.ds(pl.multiple_of(h * D, D), D)], preferred_element_type=jnp.float32
                    )
                out[:, cols(h)] = value.astype(jnp.bfloat16)
            put(chunk_index * CH)

        for step in (4, 3, 5, 2, 6, 1, 7):
            gz(step).start()
        for i in range(NZ + 2):
            if i < NZ:
                step = ORDER[i]
                if step:
                    gz(step).wait_recv()
                gy(0, step).start()
                gy(1, step).start()
                if i == NZ - 1:
                    share(0, y).start()
            if 1 <= i <= NZ:
                step = ORDER[i - 1]
                gy(0, step).wait_recv()
                gy(1, step).wait_recv()
                relay(step).start()
                if i == NZ:
                    share(1, left).start()
                    share(2, right).start()
            if i >= 2:
                step = ORDER[i - 2]
                relay(step).wait_recv()
                share_piece(step).start()
        read(c * NY + y)
        read(c * NY + left)
        read(c * NY + right)
        for j, yc in enumerate((y, left, right)):
            share(j, yc).wait_recv()
            read((1 - c) * NY + yc)
        read(c * NY + opp)
        for step in ORDER:
            share_piece(step).wait_recv()
        read((1 - c) * NY + opp)
        for step in range(NZ):
            if step:
                gz(step).wait_send()
            gy(0, step).wait_send()
            gy(1, step).wait_send()
            relay(step).wait_send()
            share_piece(step).wait_send()
        for j, yc in enumerate((y, left, right)):
            share(j, yc).wait_send()

    @pl.when(f == 0)
    def _():
        @pl.loop(0, 2 * NY)
        def _(j):
            out[:, cols(j * CH, CH)] = loc[:, cols(j * CH, CH)].astype(jnp.bfloat16)
            put(j * CH)

    @pl.when((f == 1) | (f == 2))
    def _():
        gather(1)

    @pl.when(f == 3)
    def _():
        gather(2)

    @pl.when(sending)
    def _():
        for j in range(NY):
            sib_copy(j, chunk_at(j)).wait_send()
        for cp in y_copies:
            cp.wait_send()
        for i in range(1, NZ):
            z_copy(i).wait_send()
        for src in range(3):

            @pl.when(f == src)
            def _():
                for dst in range(3, src, -1):
                    x_copy(src, dst).wait_send()

    for j in range(2 * NY):
        pltpu.make_async_copy(
            out.at[:, pl.ds(j * CR, CR)], out_hbm.at[:, pl.ds(j * CR, CR)], out_sem.at[j]
        ).wait()


def body(space_count, queries, keys, values, level_weight, frame_len, window_back):
    tok, width = queries.shape
    f32, bf16 = jnp.float32, jnp.bfloat16
    dma = pltpu.SemaphoreType.DMA
    anyspec = pl.BlockSpec(memory_space=pl.ANY)
    smem = pl.BlockSpec(memory_space=pltpu.SMEM)
    return pl.pallas_call(
        functools.partial(kernel, tok * space_count),
        out_shape=jax.ShapeDtypeStruct((tok, width), bf16),
        in_specs=[smem, smem, pl.BlockSpec(memory_space=pltpu.VMEM), anyspec, anyspec, anyspec],
        out_specs=anyspec,
        scratch_shapes=[
            pltpu.VMEM((tok, width), bf16),
            pltpu.VMEM((tok, width), bf16),
            pltpu.VMEM((tok, width), bf16),
            pltpu.VMEM((D, D), f32),
            pltpu.VMEM((D, D), f32),
            pltpu.VMEM((D, D), f32),
            pltpu.VMEM((tok, width), f32),
            pltpu.VMEM((2, tok, width), bf16),
            pltpu.VMEM((HALF * D, D), f32),
            pltpu.VMEM((HALF * D, D), bf16),
            pltpu.VMEM((HALF * D, D), bf16),
            pltpu.VMEM((6, HR, D), bf16),
            pltpu.VMEM((2, HR, D), bf16),
            pltpu.VMEM((2, CR, D), bf16),
            pltpu.VMEM((CR, D), bf16),
            pltpu.VMEM((NZ, PR, D), bf16),
            pltpu.VMEM((PR, D), bf16),
            pltpu.VMEM((3, PR, D), bf16),
            pltpu.VMEM((2, HEADS * D, D), bf16),
            pltpu.VMEM((tok, width), bf16),
            dma((5,)),
            dma((NY,)),
            dma((NY,)),
            dma((6,)),
            dma((6,)),
            dma((NZ,)),
            dma((NZ,)),
            dma((4,)),
            dma((4,)),
            dma((NZ,)),
            dma((NZ,)),
            dma((2, NZ)),
            dma((2, NZ)),
            dma((NZ,)),
            dma((NZ,)),
            dma((NZ + 3,)),
            dma((NZ + 3,)),
            dma((2 * NY,)),
        ],
        compiler_params=pltpu.CompilerParams(collective_id=0, has_side_effects=True),
    )(frame_len, window_back, level_weight, queries, keys, values)


def solution(mesh):
    return jax.shard_map(
        functools.partial(body, mesh.shape["space"]),
        mesh=mesh,
        in_specs=(
            P(("frame", "space"), None),
            P(("frame", "space"), None),
            P(("frame", "space"), None),
            P(None, None, ("frame", "space")),
            P(("frame", "space"), None),
            P(("frame", "space"), None),
        ),
        out_specs=P(("frame", "space"), None),
        check_vma=False,
    )
```

time: 333 us -> 57.6 us (0.17)
  the two profiles are of different devices: /device:TPU:7 before, /device:TPU:31 now
where the time goes in v1:
time: 57.6 us; the launch traced here: 57.4 us
  Pallas kernels  55.3 us (96%)
  local copies, waits for them, and re-layouts  2.06 us (4%)
    pallas_call x1, Pallas kernels, body(): pl.pallas_call(functools.partial(kernel, tok * space_count), out_shape=ja...  55.3 us
    unnamed x1, local copies, waits for them, and re-layouts  2.06 us

profile of v1, /device:TPU:31, one launch (start us, length us, event | category | flops | bytes accessed | tf_op | source)
XLA Modules:
  0.0 57.4 jit_solution(5440307684798048432)
XLA Ops:
  0.0 55.3 %shard_map.64 = bf16[128,3072]{1,0:T(8,128)(2,1)} custom-call(s32[1,4]{1,0:T(1,128)} %flen.1, s32[1,4]{1,0:T(1,128)} %wback.1, f32[3,24,128]{2,1,0:T(8,128)} %lw.1, bf16[128,3072]{1,0:T(8,128)(2,1)} %q_hbm.1, bf16[128,3072]{1,0:T(8,128)(2,1)} %k_hbm.1, bf16[128,3072]{1,0:T(8,128)(2,1)} %v_hbm.1), custom_call_target="tpu_custom_call" | custom-call | tf_op jit(solution)/shard_map/pallas_call | solution.py:440
  55.3 2.1 %copy.8 = bf16[128,3072]{1,0:T(8,128)(2,1)} copy(bf16[128,3072]{1,0:T(8,128)(2,1)} %shard_map.64) | data formatting | bytes 1572864

commit v2 on v1

v2 whole, which is shorter than its diff:
```python
import contextlib
import functools
import math

import jax
import jax.numpy as jnp
from jax import lax
from jax.experimental import pallas as pl
from jax.experimental.pallas import tpu as pltpu
from jax.sharding import PartitionSpec as P

MESH = pl.DeviceIdType.MESH
HEADS = 24
HALF = 12
D = 128
EPS = 1e-06
NY = 4
NZ = 8
CH = 3
CR = CH * D
HR = CR // 2
PR = CR // NZ
ORDER = (0, 1, 7, 2, 6, 3, 5, 4)
GO_RIGHT = (0, 7, 2, 5)


def scope(name):
    return contextlib.nullcontext()


def kernel(
    block_tokens,
    flen_hbm,
    wback_hbm,
    lw_hbm,
    q_hbm,
    k_hbm,
    v_hbm,
    out,
    flen,
    wback,
    lw,
    q,
    k,
    v,
    bias,
    wrows,
    wt,
    loc,
    qs,
    part,
    sib_out,
    sib_in,
    y_out,
    y_opp,
    y_in,
    z_out,
    z_in,
    x_out,
    x_in,
    lev,
    load_sem,
    misc_sem,
    step_sem,
    sib_s,
    sib_r,
    y_s,
    y_r,
    z_s,
    z_r,
    x_s,
    x_r,
    gz_s,
    gz_r,
    gy_s,
    gy_r,
    gr_s,
    gr_r,
    gs_s,
    gs_r,
):
    f = lax.axis_index("frame")
    s = lax.axis_index("space")
    c = lax.rem(s, 2)
    y = lax.rem(s // 2, NY)
    z = s // (2 * NY)
    right = lax.rem(y + 1, NY)
    left = lax.rem(y + NY - 1, NY)
    opp = lax.rem(y + 2, NY)

    def at(zz, yy, cc):
        return (zz * NY + yy) * 2 + cc

    sib = (f, at(z, y, 1 - c))
    to_right = (f, at(z, right, c))
    to_left = (f, at(z, left, c))

    def z_peer(step):
        return (f, at(lax.rem(z + step, NZ), y, c))

    def cols(head, count=1):
        return pl.ds(pl.multiple_of(head * D, D), count * D)

    def send(src, dst, ssem, rsem, dev):
        return pltpu.make_async_remote_copy(
            src_ref=src, dst_ref=dst, send_sem=ssem, recv_sem=rsem, device_id=dev, device_id_type=MESH
        )

    class Group:
        def __init__(self, copies):
            self.copies = copies

        def start(self):
            for cp in self.copies:
                cp.start()

        def wait_recv(self):
            for cp in self.copies:
                cp.wait_recv()

        def wait_send(self):
            for cp in self.copies:
                cp.wait_send()

    def chunk_at(j):
        return (opp, right, left, y)[j]

    def load(j, half, which):
        src, dst = ((k_hbm, k), (v_hbm, v))[which]
        side = (1 - c, c)[half]
        span = cols(side * HALF + chunk_at(j) * CH, CH)
        return pltpu.make_async_copy(src.at[:, span], dst.at[:, span], load_sem.at[j, half, which])

    for j in range(NY):
        for half in range(2):
            for which in range(2):
                load(j, half, which).start()
    small = [
        pltpu.make_async_copy(src, dst, misc_sem.at[i])
        for i, (src, dst) in enumerate(((flen_hbm, flen), (wback_hbm, wback), (lw_hbm, lw), (q_hbm, q)))
    ]
    for cp in small:
        cp.start()

    barrier = pltpu.get_barrier_semaphore()
    z_next = (z_peer(1), z_peer(NZ - 1))
    x_next = ((lax.rem(f + 1, 4), s), (lax.rem(f + 3, 4), s))

    def signal(sem, devices):
        for dev in devices:
            pl.semaphore_signal(sem, inc=1, device_id=dev, device_id_type=MESH)

    signal(barrier, (sib, to_right, to_left, *z_next, *x_next))

    col = lax.broadcasted_iota(jnp.int32, (D, D), 1)

    def weight(index):
        return jnp.sum(jnp.where(col == index, wt[...], 0.0), -1, keepdims=True)

    def state(head):
        kk = k[:, cols(head)].astype(jnp.float32)
        kn = (kk * lax.rsqrt(jnp.mean(kk * kk, -1, keepdims=True) + EPS)).astype(jnp.bfloat16)
        return lax.dot_general(
            kn, v[:, cols(head)], (((0,), (0,)), ((), ())), preferred_element_type=jnp.float32
        )

    def attend(first, last):
        @pl.loop(first, last)
        def _(j):
            for i in range(CH):
                h = j * CH + i
                qq = q[:, cols(h)]
                scores = lax.dot_general(
                    qq, k[:, cols(h)], (((1,), (1,)), ((), ())), preferred_element_type=jnp.float32
                )
                scores = scores + bias[...]
                top = jnp.max(scores, -1, keepdims=True)
                p = jnp.exp((scores - top) * (1.0 / math.sqrt(D)))
                total = jnp.sum(p, -1, keepdims=True)
                mix = jnp.dot(p.astype(jnp.bfloat16), v[:, cols(h)], preferred_element_type=jnp.float32)
                loc[:, cols(h)] = mix * (weight(h) / total)
                q32 = qq.astype(jnp.float32)
                r = lax.rsqrt(jnp.mean(q32 * q32, -1, keepdims=True) + EPS)
                qs[0, :, cols(h)] = (q32 * (r * weight(HEADS + h))).astype(jnp.bfloat16)
                qs[1, :, cols(h)] = (q32 * (r * weight(2 * HEADS + h))).astype(jnp.bfloat16)

    def rows(chunk, first=0, count=CR):
        return pl.ds(pl.multiple_of(chunk * CR + first, PR), count)

    def sib_copy(j, yc):
        return send(sib_out.at[rows(yc)], sib_in.at[rows(yc)], sib_s.at[j], sib_r.at[j], sib)


    y_copies = [
        send(y_out.at[0], y_opp.at[0], y_s.at[0], y_r.at[0], to_right),
        send(y_out.at[1], y_opp.at[1], y_s.at[1], y_r.at[1], to_left),
        send(y_out.at[2], y_in.at[0, pl.ds(HR, HR)], y_s.at[2], y_r.at[2], to_right),
        send(y_out.at[3], y_in.at[1, pl.ds(0, HR)], y_s.at[3], y_r.at[3], to_left),
        send(y_out.at[4], y_in.at[0, pl.ds(0, HR)], y_s.at[4], y_r.at[4], to_right),
        send(y_out.at[5], y_in.at[1, pl.ds(HR, HR)], y_s.at[5], y_r.at[5], to_left),
    ]

    def z_copy(step):
        dst_z = lax.rem(z + step, NZ)
        return send(
            z_out.at[pl.ds(pl.multiple_of(dst_z * PR, PR), PR)],
            z_in.at[step],
            z_s.at[step],
            z_r.at[step],
            z_peer(step),
        )

    def x_copy(src_f, dst_f):
        return send(x_out, x_in.at[src_f], x_s.at[dst_f], x_r.at[src_f], (dst_f, s))

    sending = f < 3

    def states(j, half):
        with scope("st"):
            load(j, half, 0).wait()
            load(j, half, 1).wait()
            yc = chunk_at(j)
            side = (1 - c, c)[half]
            for i in range(CH):
                value = state(side * HALF + yc * CH + i)
                span = pl.ds(pl.multiple_of(yc * CR + i * D, D), D)
                if half == 0:
                    sib_out[span] = value.astype(jnp.bfloat16)
                else:
                    part[span] = value

    def add_sib(j):
        yc = chunk_at(j)
        with scope("sw"):
            sib_copy(j, yc).wait_recv()
        return part[rows(yc)] + sib_in[rows(yc)].astype(jnp.float32)

    def send_opp():
        total = add_sib(0).astype(jnp.bfloat16)
        y_out[0] = total[:HR]
        y_out[1] = total[HR:]
        y_copies[0].start()
        y_copies[1].start()

    def send_right():
        total = add_sib(1)
        part[rows(right)] = total
        y_out[2] = total[HR:].astype(jnp.bfloat16)
        y_copies[2].start()

    def send_left():
        total = add_sib(2)
        part[rows(left)] = total
        y_out[3] = total[:HR].astype(jnp.bfloat16)
        y_copies[3].start()

    @pl.when(sending)
    def _():
        states(0, 0)

    with scope("barrier"):
        pl.semaphore_wait(barrier, 7)
    signal(step_sem.at[0], z_next)
    signal(step_sem.at[3], x_next)

    @pl.when(sending)
    def _():
        sib_copy(0, chunk_at(0)).start()
        states(0, 1)
        states(1, 0)
        sib_copy(1, chunk_at(1)).start()
        states(1, 1)

    with scope("b1"):
        pl.semaphore_wait(step_sem.at[0], 2)
    signal(step_sem.at[1], z_next)

    @pl.when(sending)
    def _():
        send_opp()
        states(2, 0)
        sib_copy(2, chunk_at(2)).start()
        states(2, 1)
        send_right()
        states(3, 0)
        sib_copy(3, chunk_at(3)).start()
        states(3, 1)
        send_left()

    with scope("b2"):
        pl.semaphore_wait(step_sem.at[1], 2)
    signal(step_sem.at[2], z_next)

    @pl.when(sending)
    def _():
        part[rows(y)] = add_sib(3)

    @pl.when(jnp.logical_not(sending))
    def _():
        for j in range(NY):
            for half in range(2):
                load(j, half, 0).wait()
                load(j, half, 1).wait()

    for cp in small:
        cp.wait()
    row = lax.broadcasted_iota(jnp.int32, (D, D), 0)
    floor = jnp.full((D, D), 0, jnp.int32)
    start = 0
    for i in range(4):
        low = jnp.maximum(start - wback[0, i], 0)
        floor = jnp.where(row >= start, low, floor)
        start = start + flen[0, i]
    bias[...] = jnp.where((col <= row) & (col >= floor), 0.0, -jnp.inf)
    scale1 = 1.0 / math.sqrt(D * block_tokens)
    scale2 = 1.0 / math.sqrt(D * 2 * block_tokens)
    wrows[...] = jnp.zeros_like(wrows)
    wrows[0:HEADS] = lw[0]
    wrows[HEADS : 2 * HEADS] = jnp.where(f == 2, lw[2] * scale2, lw[1] * scale1)
    wrows[2 * HEADS : 3 * HEADS] = lw[2] * scale2
    wt[...] = jnp.transpose(wrows[...])

    with scope("att0"):
        attend(0, 2)

    @pl.when(sending)
    def _():
        with scope("yw"):
            y_copies[0].wait_recv()
        y_out[4] = (part[rows(right, 0, HR)] + y_opp[0].astype(jnp.float32)).astype(jnp.bfloat16)
        y_copies[4].start()
        with scope("yw"):
            y_copies[1].wait_recv()
        y_out[5] = (part[rows(left, HR, HR)] + y_opp[1].astype(jnp.float32)).astype(jnp.bfloat16)
        y_copies[5].start()

    with scope("att1"):
        attend(2, 4)
    with scope("b3"):
        pl.semaphore_wait(step_sem.at[2], 2)
        pl.semaphore_wait(step_sem.at[3], 2)

    @pl.when(sending)
    def _():
        with scope("yw2"):
            for i in range(2, 6):
                y_copies[i].wait_recv()
        total = part[rows(y)] + y_in[0].astype(jnp.float32) + y_in[1].astype(jnp.float32)
        part[rows(y)] = total
        z_out[...] = total.astype(jnp.bfloat16)
        for i in (4, 3, 5, 2, 6, 1, 7):
            z_copy(i).start()

    with scope("att2"):
        attend(4, 8)

    @pl.when(sending)
    def _():
        total = part[pl.ds(pl.multiple_of(y * CR + z * PR, PR), PR)]
        for i in range(1, NZ):
            with scope("zw"):
                z_copy(i).wait_recv()
            total = total + z_in[i].astype(jnp.float32)
        x_out[...] = total.astype(jnp.bfloat16)

        for src in range(3):

            @pl.when(f == src)
            def _():
                for dst in range(3, src, -1):
                    x_copy(src, dst).start()

    chunk = c * NY + y
    piece = pl.ds(pl.multiple_of(chunk * CR + z * PR, PR), PR)

    @pl.when(f == 1)
    def _():
        with scope("xw"):
            x_copy(0, 1).wait_recv()
        lev[0, piece] = x_in[0]

    @pl.when(f == 2)
    def _():
        with scope("xw"):
            x_copy(0, 2).wait_recv()
        with scope("xw"):
            x_copy(1, 2).wait_recv()
        lev[0, piece] = (x_in[0].astype(jnp.float32) + x_in[1].astype(jnp.float32)).astype(jnp.bfloat16)

    @pl.when(f == 3)
    def _():
        for src in range(3):
            with scope("xw"):
                x_copy(src, 3).wait_recv()
        lev[0, piece] = x_in[2]
        lev[1, piece] = (x_in[0].astype(jnp.float32) + x_in[1].astype(jnp.float32)).astype(jnp.bfloat16)

    def gather(n):
        def move(at_row, count, ssem, rsem, dev):
            span = pl.ds(pl.multiple_of(at_row, PR), count)
            return Group(
                [send(lev.at[m, span], lev.at[m, span], ssem.at[m], rsem.at[m], dev) for m in range(n)]
            )

        def at_piece(yc, step):
            return (c * NY + yc) * CR + lax.rem(z + NZ - step, NZ) * PR

        def gz(step):
            return move(at_piece(y, 0), PR, gz_s.at[step], gz_r.at[step], z_peer(step))

        def gy(side, step):
            dev = to_right if side == 0 else to_left
            return move(at_piece(y, step), PR, gy_s.at[side, step], gy_r.at[side, step], dev)

        def relay(step):
            if step in GO_RIGHT:
                return move(at_piece(left, step), PR, gr_s.at[step], gr_r.at[step], to_right)
            return move(at_piece(right, step), PR, gr_s.at[step], gr_r.at[step], to_left)

        def share(j, yc):
            return move((c * NY + yc) * CR, CR, gs_s.at[j], gs_r.at[j], sib)

        def share_piece(step):
            return move(at_piece(opp, step), PR, gs_s.at[3 + step], gs_r.at[3 + step], sib)

        def read(chunk_index):
            for i in range(CH):
                h = chunk_index * CH + i
                value = loc[:, cols(h)]
                for m in range(n):
                    value = value + jnp.dot(
                        qs[m, :, cols(h)], lev[m, pl.ds(pl.multiple_of(h * D, D), D)], preferred_element_type=jnp.float32
                    )
                out[:, cols(h)] = value.astype(jnp.bfloat16)

        for step in (4, 3, 5, 2, 6, 1, 7):
            gz(step).start()
        for step in ORDER:
            if step:
                with scope("gzw%d" % step):
                    gz(step).wait_recv()
            gy(0, step).start()
            gy(1, step).start()
        share(0, y).start()
        read(c * NY + y)
        for step in ORDER:
            with scope("gyw%d" % step):
                gy(0, step).wait_recv()
                gy(1, step).wait_recv()
            relay(step).start()
        share(1, left).start()
        share(2, right).start()
        with scope("sw0"):
            share(0, y).wait_recv()
        read((1 - c) * NY + y)
        read(c * NY + left)
        read(c * NY + right)
        for step in ORDER:
            with scope("grw%d" % step):
                relay(step).wait_recv()
            share_piece(step).start()
        for j, yc in ((1, left), (2, right)):
            with scope("sw%d" % j):
                share(j, yc).wait_recv()
            read((1 - c) * NY + yc)
        read(c * NY + opp)
        for step in ORDER:
            with scope("gsw%d" % step):
                share_piece(step).wait_recv()
        read((1 - c) * NY + opp)
        for step in range(NZ):
            if step:
                gz(step).wait_send()
            gy(0, step).wait_send()
            gy(1, step).wait_send()
            relay(step).wait_send()
            share_piece(step).wait_send()
        for j, yc in enumerate((y, left, right)):
            share(j, yc).wait_send()

    @pl.when(f == 0)
    def _():
        @pl.loop(0, 2 * NY)
        def _(j):
            out[:, cols(j * CH, CH)] = loc[:, cols(j * CH, CH)].astype(jnp.bfloat16)

    @pl.when((f == 1) | (f == 2))
    def _():
        gather(1)

    @pl.when(f == 3)
    def _():
        gather(2)

    @pl.when(sending)
    def _():
        for j in range(NY):
            sib_copy(j, chunk_at(j)).wait_send()
        for cp in y_copies:
            cp.wait_send()
        for i in range(1, NZ):
            z_copy(i).wait_send()
        for src in range(3):

            @pl.when(f == src)
            def _():
                for dst in range(3, src, -1):
                    x_copy(src, dst).wait_send()


def body(space_count, queries, keys, values, level_weight, frame_len, window_back):
    tok, width = queries.shape
    f32, bf16 = jnp.float32, jnp.bfloat16
    dma = pltpu.SemaphoreType.DMA
    anyspec = pl.BlockSpec(memory_space=pl.ANY)
    return pl.pallas_call(
        functools.partial(kernel, tok * space_count),
        out_shape=pltpu.VMEM((tok, width), bf16),
        in_specs=[anyspec] * 6,
        out_specs=pl.BlockSpec(memory_space=pltpu.VMEM),
        scratch_shapes=[
            pltpu.SMEM((1, 4), jnp.int32),
            pltpu.SMEM((1, 4), jnp.int32),
            pltpu.VMEM(level_weight.shape, f32),
            pltpu.VMEM((tok, width), bf16),
            pltpu.VMEM((tok, width), bf16),
            pltpu.VMEM((tok, width), bf16),
            pltpu.VMEM((D, D), f32),
            pltpu.VMEM((D, D), f32),
            pltpu.VMEM((D, D), f32),
            pltpu.VMEM((tok, width), f32),
            pltpu.VMEM((2, tok, width), bf16),
            pltpu.VMEM((HALF * D, D), f32),
            pltpu.VMEM((HALF * D, D), bf16),
            pltpu.VMEM((HALF * D, D), bf16),
            pltpu.VMEM((6, HR, D), bf16),
            pltpu.VMEM((2, HR, D), bf16),
            pltpu.VMEM((2, CR, D), bf16),
            pltpu.VMEM((CR, D), bf16),
            pltpu.VMEM((NZ, PR, D), bf16),
            pltpu.VMEM((PR, D), bf16),
            pltpu.VMEM((3, PR, D), bf16),
            pltpu.VMEM((2, HEADS * D, D), bf16),
            dma((NY, 2, 2)),
            dma((4,)),
            pltpu.SemaphoreType.REGULAR((4,)),
            dma((NY,)),
            dma((NY,)),
            dma((6,)),
            dma((6,)),
            dma((NZ,)),
            dma((NZ,)),
            dma((4,)),
            dma((4,)),
            dma((NZ, 2)),
            dma((NZ, 2)),
            dma((2, NZ, 2)),
            dma((2, NZ, 2)),
            dma((NZ, 2)),
            dma((NZ, 2)),
            dma((NZ + 3, 2)),
            dma((NZ + 3, 2)),
        ],
        compiler_params=pltpu.CompilerParams(collective_id=0, has_side_effects=True),
    )(frame_len, window_back, level_weight, queries, keys, values)


def solution(mesh):
    return jax.shard_map(
        functools.partial(body, mesh.shape["space"]),
        mesh=mesh,
        in_specs=(
            P(("frame", "space"), None),
            P(("frame", "space"), None),
            P(("frame", "space"), None),
            P(None, None, ("frame", "space")),
            P(("frame", "space"), None),
            P(("frame", "space"), None),
        ),
        out_specs=P(("frame", "space"), None),
        check_vma=False,
    )
```

time: 57.6 us -> 43.3 us (0.75)
  the two profiles are of different devices: /device:TPU:31 before, /device:TPU:7 now
where the time goes in v2:
time: 43.3 us; the launch traced here: 43.2 us
  Pallas kernels  42.3 us (98%)
  local copies, waits for them, and re-layouts  0.88 us (2%)
    pallas_call x1, Pallas kernels, body(): pl.pallas_call(functools.partial(kernel, tok * space_count), out_shape=pl...  42.3 us
    unnamed x1, local copies, waits for them, and re-layouts  0.88 us

profile of v2, /device:TPU:7, one launch (start us, length us, event | category | flops | bytes accessed | tf_op | source)
XLA Modules:
  0.0 43.2 jit_solution(369393934738693626)
XLA Ops:
  0.0 42.3 %shard_map.64 = bf16[128,3072]{1,0:T(8,128)(2,1)S(1)} custom-call(s32[1,4]{1,0:T(1,128)} %flen_hbm.1, s32[1,4]{1,0:T(1,128)} %wback_hbm.1, f32[3,24,128]{2,1,0:T(8,128)} %lw_hbm.1, bf16[128,3072]{1,0:T(8,128)(2,1)} %q_hbm.1, bf16[128,3072]{1,0:T(8,128)(2,1)} %k_hbm.1, bf16[128,3072]{1,0:T(8,128)(2,1)} %v_hbm.1), custom_call_target="tpu_custom_call" | custom-call | tf_op jit(solution)/shard_map/pallas_call | solution.py:516
  42.3 0.9 %copy.8 = bf16[128,3072]{1,0:T(8,128)(2,1)} copy(bf16[128,3072]{1,0:T(8,128)(2,1)S(1)} %shard_map.64) | data formatting | bytes 1572864

commit v3 on v2

--- a/solution.py
+++ b/solution.py
@@ -18,10 +18,8 @@
 NZ = 8
 CH = 3
 CR = CH * D
-HR = CR // 2
 PR = CR // NZ
 ORDER = (0, 1, 7, 2, 6, 3, 5, 4)
-GO_RIGHT = (0, 7, 2, 5)
 
 
 def scope(name):
@@ -52,7 +50,6 @@
     sib_out,
     sib_in,
     y_out,
-    y_opp,
     y_in,
     z_out,
     z_in,
@@ -74,8 +71,6 @@
     gz_r,
     gy_s,
     gy_r,
-    gr_s,
-    gr_r,
     gs_s,
     gs_r,
 ):
@@ -94,6 +89,8 @@
     sib = (f, at(z, y, 1 - c))
     to_right = (f, at(z, right, c))
     to_left = (f, at(z, left, c))
+    to_opp = (f, at(z, opp, c))
+    across = ((to_opp, opp), (to_right, right), (to_left, left))
 
     def z_peer(step):
         return (f, at(lax.rem(z + step, NZ), y, c))
@@ -191,14 +188,7 @@
         return send(sib_out.at[rows(yc)], sib_in.at[rows(yc)], sib_s.at[j], sib_r.at[j], sib)
 
 
-    y_copies = [
-        send(y_out.at[0], y_opp.at[0], y_s.at[0], y_r.at[0], to_right),
-        send(y_out.at[1], y_opp.at[1], y_s.at[1], y_r.at[1], to_left),
-        send(y_out.at[2], y_in.at[0, pl.ds(HR, HR)], y_s.at[2], y_r.at[2], to_right),
-        send(y_out.at[3], y_in.at[1, pl.ds(0, HR)], y_s.at[3], y_r.at[3], to_left),
-        send(y_out.at[4], y_in.at[0, pl.ds(0, HR)], y_s.at[4], y_r.at[4], to_right),
-        send(y_out.at[5], y_in.at[1, pl.ds(HR, HR)], y_s.at[5], y_r.at[5], to_left),
-    ]
+    y_copies = [send(y_out.at[i], y_in.at[i], y_s.at[i], y_r.at[i], across[i][0]) for i in range(3)]
 
     def z_copy(step):
         dst_z = lax.rem(z + step, NZ)
@@ -235,24 +225,9 @@
             sib_copy(j, yc).wait_recv()
         return part[rows(yc)] + sib_in[rows(yc)].astype(jnp.float32)
 
-    def send_opp():
-        total = add_sib(0).astype(jnp.bfloat16)
-        y_out[0] = total[:HR]
-        y_out[1] = total[HR:]
-        y_copies[0].start()
-        y_copies[1].start()
-
-    def send_right():
-        total = add_sib(1)
-        part[rows(right)] = total
-        y_out[2] = total[HR:].astype(jnp.bfloat16)
-        y_copies[2].start()
-
-    def send_left():
-        total = add_sib(2)
-        part[rows(left)] = total
-        y_out[3] = total[:HR].astype(jnp.bfloat16)
-        y_copies[3].start()
+    def send_y(j):
+        y_out[j] = add_sib(j).astype(jnp.bfloat16)
+        y_copies[j].start()
 
     @pl.when(sending)
     def _():
@@ -261,7 +236,8 @@
     with scope("barrier"):
         pl.semaphore_wait(barrier, 7)
     signal(step_sem.at[0], z_next)
-    signal(step_sem.at[3], x_next)
+    signal(step_sem.at[3], (to_right, to_left))
+    signal(step_sem.at[4], x_next)
 
     @pl.when(sending)
     def _():
@@ -271,21 +247,27 @@
         sib_copy(1, chunk_at(1)).start()
         states(1, 1)
 
+    with scope("x1"):
+        pl.semaphore_wait(step_sem.at[3], 2)
+
+    @pl.when(sending)
+    def _():
+        send_y(0)
+
     with scope("b1"):
         pl.semaphore_wait(step_sem.at[0], 2)
     signal(step_sem.at[1], z_next)
 
     @pl.when(sending)
     def _():
-        send_opp()
         states(2, 0)
         sib_copy(2, chunk_at(2)).start()
         states(2, 1)
-        send_right()
+        send_y(1)
         states(3, 0)
         sib_copy(3, chunk_at(3)).start()
         states(3, 1)
-        send_left()
+        send_y(2)
 
     with scope("b2"):
         pl.semaphore_wait(step_sem.at[1], 2)
@@ -321,31 +303,22 @@
     wt[...] = jnp.transpose(wrows[...])
 
     with scope("att0"):
-        attend(0, 2)
-
-    @pl.when(sending)
-    def _():
-        with scope("yw"):
-            y_copies[0].wait_recv()
-        y_out[4] = (part[rows(right, 0, HR)] + y_opp[0].astype(jnp.float32)).astype(jnp.bfloat16)
-        y_copies[4].start()
-        with scope("yw"):
-            y_copies[1].wait_recv()
-        y_out[5] = (part[rows(left, HR, HR)] + y_opp[1].astype(jnp.float32)).astype(jnp.bfloat16)
-        y_copies[5].start()
+        attend(0, 1)
 
     with scope("att1"):
-        attend(2, 4)
+        attend(1, 4)
     with scope("b3"):
         pl.semaphore_wait(step_sem.at[2], 2)
-        pl.semaphore_wait(step_sem.at[3], 2)
+        pl.semaphore_wait(step_sem.at[4], 2)
 
     @pl.when(sending)
     def _():
         with scope("yw2"):
-            for i in range(2, 6):
-                y_copies[i].wait_recv()
-        total = part[rows(y)] + y_in[0].astype(jnp.float32) + y_in[1].astype(jnp.float32)
+            for cp in y_copies:
+                cp.wait_recv()
+        total = part[rows(y)]
+        for i in range(3):
+            total = total + y_in[i].astype(jnp.float32)
         part[rows(y)] = total
         z_out[...] = total.astype(jnp.bfloat16)
         for i in (4, 3, 5, 2, 6, 1, 7):
@@ -408,20 +381,16 @@
         def gz(step):
             return move(at_piece(y, 0), PR, gz_s.at[step], gz_r.at[step], z_peer(step))
 
-        def gy(side, step):
-            dev = to_right if side == 0 else to_left
-            return move(at_piece(y, step), PR, gy_s.at[side, step], gy_r.at[side, step], dev)
-
-        def relay(step):
-            if step in GO_RIGHT:
-                return move(at_piece(left, step), PR, gr_s.at[step], gr_r.at[step], to_right)
-            return move(at_piece(right, step), PR, gr_s.at[step], gr_r.at[step], to_left)
-
-        def share(j, yc):
-            return move((c * NY + yc) * CR, CR, gs_s.at[j], gs_r.at[j], sib)
-
-        def share_piece(step):
-            return move(at_piece(opp, step), PR, gs_s.at[3 + step], gs_r.at[3 + step], sib)
+        def gy(i, step):
+            return move(at_piece(y, step), PR, gy_s.at[i, step], gy_r.at[i, step], across[i][0])
+
+        source = (opp, left, right)
+
+        def share(i, step):
+            return move(at_piece(source[i], step), PR, gs_s.at[i, step], gs_r.at[i, step], sib)
+
+        def share_own():
+            return move((c * NY + y) * CR, CR, gs_s.at[3, 0], gs_r.at[3, 0], sib)
 
         def read(chunk_index):
             for i in range(CH):
@@ -433,50 +402,49 @@
                     )
                 out[:, cols(h)] = value.astype(jnp.bfloat16)
 
-        for step in (4, 3, 5, 2, 6, 1, 7):
+        def forward(*steps):
+            for step in steps:
+                if step:
+                    with scope("gzw%d" % step):
+                        gz(step).wait_recv()
+                for i in range(3):
+                    gy(i, step).start()
+
+        def pass_on(*steps):
+            for step in steps:
+                for i in range(3):
+                    with scope("gyw%d%d" % (i, step)):
+                        gy(i, step).wait_recv()
+                    share(i, step).start()
+
+        gz(1).start()
+        gz(7).start()
+        forward(0)
+        for step in (4, 2, 6, 3, 5):
             gz(step).start()
-        for step in ORDER:
-            if step:
-                with scope("gzw%d" % step):
-                    gz(step).wait_recv()
-            gy(0, step).start()
-            gy(1, step).start()
-        share(0, y).start()
+        forward(1, 7, 2, 6, 3, 5, 4)
+        share_own().start()
         read(c * NY + y)
-        for step in ORDER:
-            with scope("gyw%d" % step):
-                gy(0, step).wait_recv()
-                gy(1, step).wait_recv()
-            relay(step).start()
-        share(1, left).start()
-        share(2, right).start()
+        pass_on(0, 1, 7, 2, 6)
         with scope("sw0"):
-            share(0, y).wait_recv()
+            share_own().wait_recv()
         read((1 - c) * NY + y)
-        read(c * NY + left)
-        read(c * NY + right)
-        for step in ORDER:
-            with scope("grw%d" % step):
-                relay(step).wait_recv()
-            share_piece(step).start()
-        for j, yc in ((1, left), (2, right)):
-            with scope("sw%d" % j):
-                share(j, yc).wait_recv()
+        pass_on(3, 5, 4)
+        for yc in source:
+            read(c * NY + yc)
+        for i, yc in enumerate(source):
+            for step in ORDER:
+                with scope("gsw%d%d" % (i, step)):
+                    share(i, step).wait_recv()
             read((1 - c) * NY + yc)
-        read(c * NY + opp)
-        for step in ORDER:
-            with scope("gsw%d" % step):
-                share_piece(step).wait_recv()
-        read((1 - c) * NY + opp)
         for step in range(NZ):
             if step:
-                gz(step).wait_send()
-            gy(0, step).wait_send()
-            gy(1, step).wait_send()
-            relay(step).wait_send()
-            share_piece(step).wait_send()
-        for j, yc in enumerate((y, left, right)):
-            share(j, yc).wait_send()
+                with scope("ws"):
+                    gz(step).wait_send()
+            for i in range(3):
+                gy(i, step).wait_send()
+                share(i, step).wait_send()
+        share_own().wait_send()
 
     @pl.when(f == 0)
     def _():
@@ -495,7 +463,8 @@
     @pl.when(sending)
     def _():
         for j in range(NY):
-            sib_copy(j, chunk_at(j)).wait_send()
+            with scope('tail'):
+                sib_copy(j, chunk_at(j)).wait_send()
         for cp in y_copies:
             cp.wait_send()
         for i in range(1, NZ):
@@ -533,9 +502,8 @@
             pltpu.VMEM((HALF * D, D), f32),
             pltpu.VMEM((HALF * D, D), bf16),
             pltpu.VMEM((HALF * D, D), bf16),
-            pltpu.VMEM((6, HR, D), bf16),
-            pltpu.VMEM((2, HR, D), bf16),
-            pltpu.VMEM((2, CR, D), bf16),
+            pltpu.VMEM((3, CR, D), bf16),
+            pltpu.VMEM((3, CR, D), bf16),
             pltpu.VMEM((CR, D), bf16),
             pltpu.VMEM((NZ, PR, D), bf16),
             pltpu.VMEM((PR, D), bf16),
@@ -543,23 +511,21 @@
             pltpu.VMEM((2, HEADS * D, D), bf16),
             dma((NY, 2, 2)),
             dma((4,)),
-            pltpu.SemaphoreType.REGULAR((4,)),
+            pltpu.SemaphoreType.REGULAR((5,)),
             dma((NY,)),
             dma((NY,)),
-            dma((6,)),
-            dma((6,)),
+            dma((3,)),
+            dma((3,)),
             dma((NZ,)),
             dma((NZ,)),
             dma((4,)),
             dma((4,)),
             dma((NZ, 2)),
             dma((NZ, 2)),
-            dma((2, NZ, 2)),
-            dma((2, NZ, 2)),
-            dma((NZ, 2)),
-            dma((NZ, 2)),
-            dma((NZ + 3, 2)),
-            dma((NZ + 3, 2)),
+            dma((3, NZ, 2)),
+            dma((3, NZ, 2)),
+            dma((4, NZ, 2)),
+            dma((4, NZ, 2)),
         ],
         compiler_params=pltpu.CompilerParams(collective_id=0, has_side_effects=True),
     )(frame_len, window_back, level_weight, queries, keys, values)

time: 43.3 us -> 40 us (0.924)
  Pallas kernels: 42.3 us -> 39 us
    pallas_call x1, Pallas kernels: 42.3 us -> 39 us  [body(): pl.pallas_call(functools.partial(kernel, tok * space_count), out_shape=pl...]
where the time goes in v3:
time: 40 us; the launch traced here: 39.9 us
  Pallas kernels  39 us (98%)
  local copies, waits for them, and re-layouts  0.88 us (2%)
    pallas_call x1, Pallas kernels, body(): pl.pallas_call(functools.partial(kernel, tok * space_count), out_shape=pl...  39 us
    unnamed x1, local copies, waits for them, and re-layouts  0.88 us

profile of v3, /device:TPU:7, one launch (start us, length us, event | category | flops | bytes accessed | tf_op | source)
XLA Modules:
  0.0 39.9 jit_solution(10837356531181135652)
XLA Ops:
  0.0 39.0 %shard_map.64 = bf16[128,3072]{1,0:T(8,128)(2,1)S(1)} custom-call(s32[1,4]{1,0:T(1,128)} %flen_hbm.1, s32[1,4]{1,0:T(1,128)} %wback_hbm.1, f32[3,24,128]{2,1,0:T(8,128)} %lw_hbm.1, bf16[128,3072]{1,0:T(8,128)(2,1)} %q_hbm.1, bf16[128,3072]{1,0:T(8,128)(2,1)} %k_hbm.1, bf16[128,3072]{1,0:T(8,128)(2,1)} %v_hbm.1), custom_call_target="tpu_custom_call" | custom-call | tf_op jit(solution)/shard_map/pallas_call | solution.py:485
  39.0 0.9 %copy.8 = bf16[128,3072]{1,0:T(8,128)(2,1)} copy(bf16[128,3072]{1,0:T(8,128)(2,1)S(1)} %shard_map.64) | data formatting | bytes 1572864

commit v4 on v3

--- a/solution.py
+++ b/solution.py
@@ -20,6 +20,7 @@
 CR = CH * D
 PR = CR // NZ
 ORDER = (0, 1, 7, 2, 6, 3, 5, 4)
+DELIVER = (0, 1, 7, 4, 2, 6, 3, 5)
 
 
 def scope(name):
@@ -54,7 +55,6 @@
     z_out,
     z_in,
     x_out,
-    x_in,
     lev,
     load_sem,
     misc_sem,
@@ -65,9 +65,7 @@
     y_r,
     z_s,
     z_r,
-    x_s,
-    x_r,
-    gz_s,
+    d_s,
     gz_r,
     gy_s,
     gy_r,
@@ -92,8 +90,8 @@
     to_opp = (f, at(z, opp, c))
     across = ((to_opp, opp), (to_right, right), (to_left, left))
 
-    def z_peer(step):
-        return (f, at(lax.rem(z + step, NZ), y, c))
+    def z_peer(step, ff=f):
+        return (ff, at(lax.rem(z + step, NZ), y, c))
 
     def cols(head, count=1):
         return pl.ds(pl.multiple_of(head * D, D), count * D)
@@ -190,18 +188,32 @@
 
     y_copies = [send(y_out.at[i], y_in.at[i], y_s.at[i], y_r.at[i], across[i][0]) for i in range(3)]
 
-    def z_copy(step):
-        dst_z = lax.rem(z + step, NZ)
+    summing = c == f
+    slot = jnp.where(f == 2, 0, f)
+
+    def z_copy(step, source=slot):
+        at_row = pl.multiple_of(lax.rem(z + step, NZ) * PR, PR)
         return send(
-            z_out.at[pl.ds(pl.multiple_of(dst_z * PR, PR), PR)],
-            z_in.at[step],
+            z_out.at[pl.ds(at_row, PR)],
+            z_in.at[source, step],
             z_s.at[step],
-            z_r.at[step],
-            z_peer(step),
+            z_r.at[source, step],
+            z_peer(step, jnp.where(f == 2, 2, c)),
         )
 
-    def x_copy(src_f, dst_f):
-        return send(x_out, x_in.at[src_f], x_s.at[dst_f], x_r.at[src_f], (dst_f, s))
+    chunk = c * NY + y
+    piece = pl.ds(pl.multiple_of(chunk * CR + z * PR, PR), PR)
+
+    def deliver(step, k, target, m):
+        return send(x_out.at[k], lev.at[m, piece], d_s.at[target - 1, step], gz_r.at[m, step], z_peer(step, target))
+
+    def deliveries():
+        return (
+            ((f < 2) & summing, [(step, 1, target, target - 2) for step in DELIVER for target in (2, 3)]),
+            ((f == 0) & summing, [(step, 0, 1, 0) for step in DELIVER]),
+            ((f == 1) & summing, [(step, 0, 1, 0) for step in DELIVER if step]),
+            (f == 2, [(step, 0, 3, 0) for step in DELIVER]),
+        )
 
     sending = f < 3
 
@@ -237,7 +249,6 @@
         pl.semaphore_wait(barrier, 7)
     signal(step_sem.at[0], z_next)
     signal(step_sem.at[3], (to_right, to_left))
-    signal(step_sem.at[4], x_next)
 
     @pl.when(sending)
     def _():
@@ -304,12 +315,14 @@
 
     with scope("att0"):
         attend(0, 1)
-
+    with scope("b3"):
+        pl.semaphore_wait(step_sem.at[2], 2)
+    signal(step_sem.at[4], z_next)
     with scope("att1"):
         attend(1, 4)
-    with scope("b3"):
-        pl.semaphore_wait(step_sem.at[2], 2)
+    with scope("b4"):
         pl.semaphore_wait(step_sem.at[4], 2)
+    signal(step_sem.at[5], x_next)
 
     @pl.when(sending)
     def _():
@@ -324,127 +337,138 @@
         for i in (4, 3, 5, 2, 6, 1, 7):
             z_copy(i).start()
 
+        @pl.when((f < 2) & jnp.logical_not(summing))
+        def _():
+            z_copy(0).start()
+
     with scope("att2"):
         attend(4, 8)
 
-    @pl.when(sending)
+    with scope("b5"):
+        pl.semaphore_wait(step_sem.at[5], 2)
+
+    @pl.when((f == 2) | ((f < 2) & summing))
     def _():
         total = part[pl.ds(pl.multiple_of(y * CR + z * PR, PR), PR)]
         for i in range(1, NZ):
             with scope("zw"):
                 z_copy(i).wait_recv()
-            total = total + z_in[i].astype(jnp.float32)
-        x_out[...] = total.astype(jnp.bfloat16)
-
-        for src in range(3):
-
-            @pl.when(f == src)
-            def _():
-                for dst in range(3, src, -1):
-                    x_copy(src, dst).start()
-
-    chunk = c * NY + y
-    piece = pl.ds(pl.multiple_of(chunk * CR + z * PR, PR), PR)
-
-    @pl.when(f == 1)
-    def _():
-        with scope("xw"):
-            x_copy(0, 1).wait_recv()
-        lev[0, piece] = x_in[0]
-
-    @pl.when(f == 2)
-    def _():
-        with scope("xw"):
-            x_copy(0, 2).wait_recv()
-        with scope("xw"):
-            x_copy(1, 2).wait_recv()
-        lev[0, piece] = (x_in[0].astype(jnp.float32) + x_in[1].astype(jnp.float32)).astype(jnp.bfloat16)
-
-    @pl.when(f == 3)
-    def _():
-        for src in range(3):
-            with scope("xw"):
-                x_copy(src, 3).wait_recv()
-        lev[0, piece] = x_in[2]
-        lev[1, piece] = (x_in[0].astype(jnp.float32) + x_in[1].astype(jnp.float32)).astype(jnp.bfloat16)
+            total = total + z_in[slot, i].astype(jnp.float32)
+
+        @pl.when(f == 2)
+        def _():
+            x_out[0] = total.astype(jnp.bfloat16)
+
+        @pl.when(f < 2)
+        def _():
+            across_sum = jnp.zeros_like(total)
+            for i in range(NZ):
+                with scope("zc"):
+                    z_copy(i, 1 - slot).wait_recv()
+                across_sum = across_sum + z_in[1 - slot, i].astype(jnp.float32)
+            x_out[1] = (total + across_sum).astype(jnp.bfloat16)
+            x_out[0] = jnp.where(f == 0, total, across_sum).astype(jnp.bfloat16)
+
+    for who, what in deliveries():
+
+        @pl.when(who)
+        def _():
+            for args in what:
+                deliver(*args).start()
+
+    @pl.when((f == 1) & summing)
+    def _():
+        lev[0, piece] = x_out[0]
 
     def gather(n):
-        def move(at_row, count, ssem, rsem, dev):
+        def move(m, at_row, count, ssem, rsem, dev):
             span = pl.ds(pl.multiple_of(at_row, PR), count)
-            return Group(
-                [send(lev.at[m, span], lev.at[m, span], ssem.at[m], rsem.at[m], dev) for m in range(n)]
-            )
+            return send(lev.at[m, span], lev.at[m, span], ssem, rsem, dev)
 
         def at_piece(yc, step):
             return (c * NY + yc) * CR + lax.rem(z + NZ - step, NZ) * PR
 
-        def gz(step):
-            return move(at_piece(y, 0), PR, gz_s.at[step], gz_r.at[step], z_peer(step))
-
-        def gy(i, step):
-            return move(at_piece(y, step), PR, gy_s.at[i, step], gy_r.at[i, step], across[i][0])
+        def gz(m, step):
+            return move(m, at_piece(y, step), PR, d_s.at[m, step], gz_r.at[m, step], sib)
+
+        def gy(m, i, step):
+            return move(m, at_piece(y, step), PR, gy_s.at[m, i, step], gy_r.at[m, i, step], across[i][0])
 
         source = (opp, left, right)
 
-        def share(i, step):
-            return move(at_piece(source[i], step), PR, gs_s.at[i, step], gs_r.at[i, step], sib)
-
-        def share_own():
-            return move((c * NY + y) * CR, CR, gs_s.at[3, 0], gs_r.at[3, 0], sib)
-
-        def read(chunk_index):
+        def share(m, i, step):
+            return move(m, at_piece(source[i], step), PR, gs_s.at[m, i, step], gs_r.at[m, i, step], sib)
+
+        def share_own(m):
+            return move(m, (c * NY + y) * CR, CR, gs_s.at[m, 3, 0], gs_r.at[m, 3, 0], sib)
+
+        def read(m, chunk_index, last=True):
             for i in range(CH):
                 h = chunk_index * CH + i
-                value = loc[:, cols(h)]
-                for m in range(n):
-                    value = value + jnp.dot(
-                        qs[m, :, cols(h)], lev[m, pl.ds(pl.multiple_of(h * D, D), D)], preferred_element_type=jnp.float32
-                    )
-                out[:, cols(h)] = value.astype(jnp.bfloat16)
-
-        def forward(*steps):
+                value = loc[:, cols(h)] + jnp.dot(
+                    qs[m, :, cols(h)], lev[m, pl.ds(pl.multiple_of(h * D, D), D)], preferred_element_type=jnp.float32
+                )
+                if last:
+                    out[:, cols(h)] = value.astype(jnp.bfloat16)
+                else:
+                    loc[:, cols(h)] = value
+
+        def forward(m, *steps):
             for step in steps:
-                if step:
-                    with scope("gzw%d" % step):
-                        gz(step).wait_recv()
+                with scope("gzw%d%d" % (m, step)):
+                    if step == 0 and n == 1:
+
+                        @pl.when(jnp.logical_not((f == 1) & summing))
+                        def _():
+                            gz(m, step).wait_recv()
+
+                    else:
+                        gz(m, step).wait_recv()
                 for i in range(3):
-                    gy(i, step).start()
-
-        def pass_on(*steps):
+                    gy(m, i, step).start()
+
+        def pass_on(m, *steps):
             for step in steps:
                 for i in range(3):
-                    with scope("gyw%d%d" % (i, step)):
-                        gy(i, step).wait_recv()
-                    share(i, step).start()
-
-        gz(1).start()
-        gz(7).start()
-        forward(0)
-        for step in (4, 2, 6, 3, 5):
-            gz(step).start()
-        forward(1, 7, 2, 6, 3, 5, 4)
-        share_own().start()
-        read(c * NY + y)
-        pass_on(0, 1, 7, 2, 6)
-        with scope("sw0"):
-            share_own().wait_recv()
-        read((1 - c) * NY + y)
-        pass_on(3, 5, 4)
+                    with scope("gyw%d%d%d" % (m, i, step)):
+                        gy(m, i, step).wait_recv()
+                    share(m, i, step).start()
+
+        for m in range(n):
+            forward(m, *ORDER)
+            share_own(m).start()
+        m = n - 1
+        if n == 2:
+            pass_on(0, *ORDER)
+            for yc in (y, *source):
+                read(0, c * NY + yc, False)
+        else:
+            read(0, c * NY + y)
+        pass_on(m, *ORDER)
+        for k in range(n):
+            with scope("sw%d" % k):
+                share_own(k).wait_recv()
+            read(k, (1 - c) * NY + y, k == m)
+        if n == 2:
+            for i, yc in enumerate(source):
+                for step in ORDER:
+                    with scope("gsw0%d%d" % (i, step)):
+                        share(0, i, step).wait_recv()
+                read(0, (1 - c) * NY + yc, False)
+            read(m, c * NY + y)
         for yc in source:
-            read(c * NY + yc)
+            read(m, c * NY + yc)
         for i, yc in enumerate(source):
             for step in ORDER:
-                with scope("gsw%d%d" % (i, step)):
-                    share(i, step).wait_recv()
-            read((1 - c) * NY + yc)
-        for step in range(NZ):
-            if step:
-                with scope("ws"):
-                    gz(step).wait_send()
-            for i in range(3):
-                gy(i, step).wait_send()
-                share(i, step).wait_send()
-        share_own().wait_send()
+                with scope("gsw%d%d%d" % (m, i, step)):
+                    share(m, i, step).wait_recv()
+            read(m, (1 - c) * NY + yc)
+        for m in range(n):
+            for step in range(NZ):
+                for i in range(3):
+                    gy(m, i, step).wait_send()
+                    share(m, i, step).wait_send()
+            share_own(m).wait_send()
 
     @pl.when(f == 0)
     def _():
@@ -469,12 +493,17 @@
             cp.wait_send()
         for i in range(1, NZ):
             z_copy(i).wait_send()
-        for src in range(3):
-
-            @pl.when(f == src)
-            def _():
-                for dst in range(3, src, -1):
-                    x_copy(src, dst).wait_send()
+
+        @pl.when((f < 2) & jnp.logical_not(summing))
+        def _():
+            z_copy(0).wait_send()
+
+    for who, what in deliveries():
+
+        @pl.when(who)
+        def _():
+            for args in what:
+                deliver(*args).wait_send()
 
 
 def body(space_count, queries, keys, values, level_weight, frame_len, window_back):
@@ -505,27 +534,24 @@
             pltpu.VMEM((3, CR, D), bf16),
             pltpu.VMEM((3, CR, D), bf16),
             pltpu.VMEM((CR, D), bf16),
-            pltpu.VMEM((NZ, PR, D), bf16),
-            pltpu.VMEM((PR, D), bf16),
-            pltpu.VMEM((3, PR, D), bf16),
+            pltpu.VMEM((2, NZ, PR, D), bf16),
+            pltpu.VMEM((2, PR, D), bf16),
             pltpu.VMEM((2, HEADS * D, D), bf16),
             dma((NY, 2, 2)),
             dma((4,)),
-            pltpu.SemaphoreType.REGULAR((5,)),
+            pltpu.SemaphoreType.REGULAR((6,)),
             dma((NY,)),
             dma((NY,)),
             dma((3,)),
             dma((3,)),
             dma((NZ,)),
-            dma((NZ,)),
-            dma((4,)),
-            dma((4,)),
-            dma((NZ, 2)),
-            dma((NZ, 2)),
-            dma((3, NZ, 2)),
-            dma((3, NZ, 2)),
-            dma((4, NZ, 2)),
-            dma((4, NZ, 2)),
+            dma((2, NZ)),
+            dma((3, NZ)),
+            dma((2, NZ)),
+            dma((2, 3, NZ)),
+            dma((2, 3, NZ)),
+            dma((2, 4, NZ)),
+            dma((2, 4, NZ)),
         ],
         compiler_params=pltpu.CompilerParams(collective_id=0, has_side_effects=True),
     )(frame_len, window_back, level_weight, queries, keys, values)

time: 40 us -> 38.3 us (0.957)
  Pallas kernels: 39 us -> 37.3 us
    pallas_call x1, Pallas kernels: 39 us -> 37.3 us  [body(): pl.pallas_call(functools.partial(kernel, tok * space_count), out_shape=pl...]
where the time goes in v4:
time: 38.3 us; the launch traced here: 38.2 us
  Pallas kernels  37.3 us (97%)
  local copies, waits for them, and re-layouts  0.88 us (2%)
    pallas_call x1, Pallas kernels, body(): pl.pallas_call(functools.partial(kernel, tok * space_count), out_shape=pl...  37.3 us
    unnamed x1, local copies, waits for them, and re-layouts  0.88 us

profile of v4, /device:TPU:7, one launch (start us, length us, event | category | flops | bytes accessed | tf_op | source)
XLA Modules:
  0.0 38.2 jit_solution(2639071703298735652)
XLA Ops:
  0.0 37.3 %shard_map.64 = bf16[128,3072]{1,0:T(8,128)(2,1)S(1)} custom-call(s32[1,4]{1,0:T(1,128)} %flen_hbm.1, s32[1,4]{1,0:T(1,128)} %wback_hbm.1, f32[3,24,128]{2,1,0:T(8,128)} %lw_hbm.1, bf16[128,3072]{1,0:T(8,128)(2,1)} %q_hbm.1, bf16[128,3072]{1,0:T(8,128)(2,1)} %k_hbm.1, bf16[128,3072]{1,0:T(8,128)(2,1)} %v_hbm.1), custom_call_target="tpu_custom_call" | custom-call | tf_op jit(solution)/shard_map/pallas_call | solution.py:514
  37.4 0.9 %copy.8 = bf16[128,3072]{1,0:T(8,128)(2,1)} copy(bf16[128,3072]{1,0:T(8,128)(2,1)S(1)} %shard_map.64) | data formatting | bytes 1572864

commit v5 on v4

--- a/solution.py
+++ b/solution.py
@@ -19,8 +19,12 @@
 CH = 3
 CR = CH * D
 PR = CR // NZ
+PA = 32
+PB = PR - PA
 ORDER = (0, 1, 7, 2, 6, 3, 5, 4)
-DELIVER = (0, 1, 7, 4, 2, 6, 3, 5)
+DELIVER = (0, 4, 1, 3, 5, 7, 2, 6)
+GROUPS = ((0,), (1, 7), (2, 6), (3, 5, 4))
+GROUP = (0, 1, 2, 3, 3, 3, 2, 1)
 
 
 def scope(name):
@@ -59,17 +63,14 @@
     load_sem,
     misc_sem,
     step_sem,
-    sib_s,
+    sent,
     sib_r,
-    y_s,
     y_r,
-    z_s,
     z_r,
-    d_s,
     gz_r,
-    gy_s,
+    gb_r,
     gy_r,
-    gs_s,
+    zb_r,
     gs_r,
 ):
     f = lax.axis_index("frame")
@@ -124,7 +125,11 @@
         src, dst = ((k_hbm, k), (v_hbm, v))[which]
         side = (1 - c, c)[half]
         span = cols(side * HALF + chunk_at(j) * CH, CH)
-        return pltpu.make_async_copy(src.at[:, span], dst.at[:, span], load_sem.at[j, half, which])
+        return pltpu.make_async_copy(src.at[:, span], dst.at[:, span], load_sem.at[j, half])
+
+    def loaded(j, half):
+        both = k.at[:, pl.ds(0, 2 * CR)]
+        pltpu.make_async_copy(k_hbm.at[:, pl.ds(0, 2 * CR)], both, load_sem.at[j, half]).wait()
 
     for j in range(NY):
         for half in range(2):
@@ -179,14 +184,18 @@
                 qs[0, :, cols(h)] = (q32 * (r * weight(HEADS + h))).astype(jnp.bfloat16)
                 qs[1, :, cols(h)] = (q32 * (r * weight(2 * HEADS + h))).astype(jnp.bfloat16)
 
+    def group(count, sem):
+        whole = sib_in.at[pl.ds(0, count)]
+        return send(whole, whole, sem, sem, sib)
+
     def rows(chunk, first=0, count=CR):
         return pl.ds(pl.multiple_of(chunk * CR + first, PR), count)
 
     def sib_copy(j, yc):
-        return send(sib_out.at[rows(yc)], sib_in.at[rows(yc)], sib_s.at[j], sib_r.at[j], sib)
-
-
-    y_copies = [send(y_out.at[i], y_in.at[i], y_s.at[i], y_r.at[i], across[i][0]) for i in range(3)]
+        return send(sib_out.at[rows(yc)], sib_in.at[rows(yc)], sent.at[0], sib_r.at[j], sib)
+
+
+    y_copies = [send(y_out.at[i], y_in.at[i], sent.at[1], y_r.at[0], across[i][0]) for i in range(3)]
 
     summing = c == f
     slot = jnp.where(f == 2, 0, f)
@@ -196,31 +205,51 @@
         return send(
             z_out.at[pl.ds(at_row, PR)],
             z_in.at[source, step],
-            z_s.at[step],
-            z_r.at[source, step],
+            sent.at[2],
+            z_r.at[source],
             z_peer(step, jnp.where(f == 2, 2, c)),
         )
 
     chunk = c * NY + y
-    piece = pl.ds(pl.multiple_of(chunk * CR + z * PR, PR), PR)
 
     def deliver(step, k, target, m):
-        return send(x_out.at[k], lev.at[m, piece], d_s.at[target - 1, step], gz_r.at[m, step], z_peer(step, target))
+        rows_a = pl.ds(0, PA)
+        return send(
+            x_out.at[k, rows_a],
+            lev.at[m, chunk, z, rows_a],
+            sent.at[2 + target],
+            gz_r.at[m, GROUP[step]],
+            z_peer(step, target),
+        )
+
+    def deliver_b(step, k, target, m):
+        rows_b = pl.ds(PA, PB)
+        return send(
+            x_out.at[k, rows_b],
+            lev.at[m, chunk, z, rows_b],
+            sent.at[2 + target],
+            gb_r.at[m],
+            (target, at(z, lax.rem(y + step, NY), c)),
+        )
 
     def deliveries():
+        def both(pairs, first=0):
+            return [deliver_b(step, *p) for step in (2, 1, 3, 0)[: NY - first] for p in pairs] + [
+                deliver(step, *p) for step in DELIVER if step >= first for p in pairs
+            ]
+
         return (
-            ((f < 2) & summing, [(step, 1, target, target - 2) for step in DELIVER for target in (2, 3)]),
-            ((f == 0) & summing, [(step, 0, 1, 0) for step in DELIVER]),
-            ((f == 1) & summing, [(step, 0, 1, 0) for step in DELIVER if step]),
-            (f == 2, [(step, 0, 3, 0) for step in DELIVER]),
+            ((f == 0) & summing, lambda: both(((1, 3, 1), (1, 2, 0), (0, 1, 0)))),
+            ((f == 1) & summing, lambda: both(((1, 3, 1), (1, 2, 0)))),
+            ((f == 1) & summing, lambda: both(((0, 1, 0),), 1)),
+            (f == 2, lambda: both(((0, 3, 0),))),
         )
 
     sending = f < 3
 
     def states(j, half):
         with scope("st"):
-            load(j, half, 0).wait()
-            load(j, half, 1).wait()
+            loaded(j, half)
             yc = chunk_at(j)
             side = (1 - c, c)[half]
             for i in range(CH):
@@ -292,8 +321,7 @@
     def _():
         for j in range(NY):
             for half in range(2):
-                load(j, half, 0).wait()
-                load(j, half, 1).wait()
+                loaded(j, half)
 
     for cp in small:
         cp.wait()
@@ -322,13 +350,11 @@
         attend(1, 4)
     with scope("b4"):
         pl.semaphore_wait(step_sem.at[4], 2)
-    signal(step_sem.at[5], x_next)
 
     @pl.when(sending)
     def _():
         with scope("yw2"):
-            for cp in y_copies:
-                cp.wait_recv()
+            group(3 * CR, y_r.at[0]).wait_recv()
         total = part[rows(y)]
         for i in range(3):
             total = total + y_in[i].astype(jnp.float32)
@@ -341,6 +367,7 @@
         def _():
             z_copy(0).start()
 
+    signal(step_sem.at[5], x_next)
     with scope("att2"):
         attend(4, 8)
 
@@ -350,9 +377,9 @@
     @pl.when((f == 2) | ((f < 2) & summing))
     def _():
         total = part[pl.ds(pl.multiple_of(y * CR + z * PR, PR), PR)]
+        with scope("zw"):
+            group((NZ - 1) * PR, z_r.at[slot]).wait_recv()
         for i in range(1, NZ):
-            with scope("zw"):
-                z_copy(i).wait_recv()
             total = total + z_in[slot, i].astype(jnp.float32)
 
         @pl.when(f == 2)
@@ -362,9 +389,9 @@
         @pl.when(f < 2)
         def _():
             across_sum = jnp.zeros_like(total)
+            with scope("zc"):
+                group(CR, z_r.at[1 - slot]).wait_recv()
             for i in range(NZ):
-                with scope("zc"):
-                    z_copy(i, 1 - slot).wait_recv()
                 across_sum = across_sum + z_in[1 - slot, i].astype(jnp.float32)
             x_out[1] = (total + across_sum).astype(jnp.bfloat16)
             x_out[0] = jnp.where(f == 0, total, across_sum).astype(jnp.bfloat16)
@@ -373,102 +400,125 @@
 
         @pl.when(who)
         def _():
-            for args in what:
-                deliver(*args).start()
+            for cp in what():
+                cp.start()
 
     @pl.when((f == 1) & summing)
     def _():
-        lev[0, piece] = x_out[0]
+        lev[0, chunk, z] = x_out[0]
 
     def gather(n):
-        def move(m, at_row, count, ssem, rsem, dev):
-            span = pl.ds(pl.multiple_of(at_row, PR), count)
-            return send(lev.at[m, span], lev.at[m, span], ssem, rsem, dev)
-
-        def at_piece(yc, step):
-            return (c * NY + yc) * CR + lax.rem(z + NZ - step, NZ) * PR
-
-        def gz(m, step):
-            return move(m, at_piece(y, step), PR, d_s.at[m, step], gz_r.at[m, step], sib)
+        def same(part, ssem, rsem, dev):
+            return send(part, part, ssem, rsem, dev)
+
+        def part_a(m, yc, step):
+            return lev.at[m, c * NY + yc, lax.rem(z + NZ - step, NZ), pl.ds(0, PA)]
+
+        def part_b(m, step):
+            return lev.at[m, pl.ds(c * NY, NY), lax.rem(z + NZ - step, NZ), pl.ds(PA, PB)]
 
         def gy(m, i, step):
-            return move(m, at_piece(y, step), PR, gy_s.at[m, i, step], gy_r.at[m, i, step], across[i][0])
+            return same(part_a(m, y, step), sent.at[6 + m], gy_r.at[m, GROUP[step]], across[i][0])
+
+        def gzb(m, step):
+            return same(part_b(m, 0), sent.at[6 + m], zb_r.at[m, GROUP[step]], z_peer(step))
 
         source = (opp, left, right)
 
-        def share(m, i, step):
-            return move(m, at_piece(source[i], step), PR, gs_s.at[m, i, step], gs_r.at[m, i, step], sib)
-
-        def share_own(m):
-            return move(m, (c * NY + y) * CR, CR, gs_s.at[m, 3, 0], gs_r.at[m, 3, 0], sib)
+        def share(part, m):
+            same(part, sent.at[8 + m], gs_r.at[m], sib).start()
 
         def read(m, chunk_index, last=True):
+            level = lev[m, chunk_index].reshape(CR, D)
             for i in range(CH):
                 h = chunk_index * CH + i
                 value = loc[:, cols(h)] + jnp.dot(
-                    qs[m, :, cols(h)], lev[m, pl.ds(pl.multiple_of(h * D, D), D)], preferred_element_type=jnp.float32
+                    qs[m, :, cols(h)], level[i * D : (i + 1) * D], preferred_element_type=jnp.float32
                 )
                 if last:
                     out[:, cols(h)] = value.astype(jnp.bfloat16)
                 else:
                     loc[:, cols(h)] = value
 
-        def forward(m, *steps):
-            for step in steps:
-                with scope("gzw%d%d" % (m, step)):
-                    if step == 0 and n == 1:
-
-                        @pl.when(jnp.logical_not((f == 1) & summing))
-                        def _():
-                            gz(m, step).wait_recv()
-
+        def unless_kept(some, rest):
+            if n == 2:
+                some()
+            else:
+                kept = (f == 1) & summing
+                pl.when(jnp.logical_not(kept))(some)
+                if rest is not None:
+                    pl.when(kept)(rest)
+
+        def forward(m, *which):
+            for g in which:
+                with scope("gzw%d%d" % (m, g)):
+                    wait = lambda: group(PA * len(GROUPS[g]), gz_r.at[m, g]).wait_recv()
+                    if g:
+                        wait()
                     else:
-                        gz(m, step).wait_recv()
-                for i in range(3):
-                    gy(m, i, step).start()
-
-        def pass_on(m, *steps):
-            for step in steps:
-                for i in range(3):
-                    with scope("gyw%d%d%d" % (m, i, step)):
-                        gy(m, i, step).wait_recv()
-                    share(m, i, step).start()
+                        unless_kept(wait, None)
+                for step in GROUPS[g]:
+                    for i in range(3):
+                        gy(m, i, step).start()
+
+        def forward_b(m):
+            with scope("gbw%d" % m):
+                unless_kept(
+                    lambda: group(NY * PB, gb_r.at[m]).wait_recv(),
+                    lambda: group((NY - 1) * PB, gb_r.at[m]).wait_recv(),
+                )
+            for step in (4, 3, 5, 2, 6, 1, 7):
+                gzb(m, step).start()
+            share(part_b(m, 0), m)
+
+        def pass_on(m, g):
+            with scope("gyw%d%d" % (m, g)):
+                group(3 * PA * len(GROUPS[g]), gy_r.at[m, g]).wait_recv()
+            for step in GROUPS[g]:
+                for yc in source:
+                    share(part_a(m, yc, step), m)
+
+        def pass_on_b(m, g):
+            with scope("zbw%d%d" % (m, g)):
+                group(NY * PB * len(GROUPS[g]), zb_r.at[m, g]).wait_recv()
+            for step in GROUPS[g]:
+                share(part_b(m, step), m)
+
+        def shared(m):
+            with scope("gsw%d" % m):
+                group(HALF * D, gs_r.at[m]).wait_recv()
 
         for m in range(n):
-            forward(m, *ORDER)
-            share_own(m).start()
+            forward(m, 0, 1)
+            forward_b(m)
+            forward(m, 2, 3)
+            share(lev.at[m, c * NY + y, pl.ds(0, NZ), pl.ds(0, PA)], m)
         m = n - 1
+        own = [c * NY + yc for yc in (y, *source)]
+        others = [(1 - c) * NY + yc for yc in (y, *source)]
+        for k in range(n):
+            pass_on(k, 0)
+            pass_on(k, 1)
+            pass_on_b(k, 1)
+            pass_on_b(k, 2)
+            pass_on(k, 2)
+            pass_on_b(k, 3)
+            pass_on(k, 3)
+            for index in own:
+                if k < m:
+                    read(k, index, False)
         if n == 2:
-            pass_on(0, *ORDER)
-            for yc in (y, *source):
-                read(0, c * NY + yc, False)
-        else:
-            read(0, c * NY + y)
-        pass_on(m, *ORDER)
+            shared(0)
+            for index in others:
+                read(0, index, False)
+        for index in own:
+            read(m, index)
+        shared(m)
+        for index in others:
+            read(m, index)
         for k in range(n):
-            with scope("sw%d" % k):
-                share_own(k).wait_recv()
-            read(k, (1 - c) * NY + y, k == m)
-        if n == 2:
-            for i, yc in enumerate(source):
-                for step in ORDER:
-                    with scope("gsw0%d%d" % (i, step)):
-                        share(0, i, step).wait_recv()
-                read(0, (1 - c) * NY + yc, False)
-            read(m, c * NY + y)
-        for yc in source:
-            read(m, c * NY + yc)
-        for i, yc in enumerate(source):
-            for step in ORDER:
-                with scope("gsw%d%d%d" % (m, i, step)):
-                    share(m, i, step).wait_recv()
-            read(m, (1 - c) * NY + yc)
-        for m in range(n):
-            for step in range(NZ):
-                for i in range(3):
-                    gy(m, i, step).wait_send()
-                    share(m, i, step).wait_send()
-            share_own(m).wait_send()
+            group(3 * NZ * PA + (NZ - 1) * NY * PB, sent.at[6 + k]).wait_send()
+            group(HALF * D, sent.at[8 + k]).wait_send()
 
     @pl.when(f == 0)
     def _():
@@ -486,24 +536,31 @@
 
     @pl.when(sending)
     def _():
-        for j in range(NY):
-            with scope('tail'):
-                sib_copy(j, chunk_at(j)).wait_send()
-        for cp in y_copies:
-            cp.wait_send()
-        for i in range(1, NZ):
-            z_copy(i).wait_send()
-
-        @pl.when((f < 2) & jnp.logical_not(summing))
+        with scope("tail"):
+            group(HALF * D, sent.at[0]).wait_send()
+        group(3 * CR, sent.at[1]).wait_send()
+        keeps = (f == 2) | summing
+
+        @pl.when(keeps)
         def _():
-            z_copy(0).wait_send()
-
-    for who, what in deliveries():
+            group((NZ - 1) * PR, sent.at[2]).wait_send()
+
+        @pl.when(jnp.logical_not(keeps))
+        def _():
+            group(CR, sent.at[2]).wait_send()
+
+    everywhere = NZ * PA + NY * PB
+    for who, target, count in (
+        ((f < 2) & summing, 2, everywhere),
+        ((f < 2) & summing, 3, everywhere),
+        ((f == 0) & summing, 1, everywhere),
+        ((f == 1) & summing, 1, everywhere - PR),
+        (f == 2, 3, everywhere),
+    ):
 
         @pl.when(who)
         def _():
-            for args in what:
-                deliver(*args).wait_send()
+            group(count, sent.at[2 + target]).wait_send()
 
 
 def body(space_count, queries, keys, values, level_weight, frame_len, window_back):
@@ -536,22 +593,19 @@
             pltpu.VMEM((CR, D), bf16),
             pltpu.VMEM((2, NZ, PR, D), bf16),
             pltpu.VMEM((2, PR, D), bf16),
-            pltpu.VMEM((2, HEADS * D, D), bf16),
-            dma((NY, 2, 2)),
+            pltpu.VMEM((2, 2 * NY, NZ, PR, D), bf16),
+            dma((NY, 2)),
             dma((4,)),
             pltpu.SemaphoreType.REGULAR((6,)),
+            dma((10,)),
             dma((NY,)),
-            dma((NY,)),
-            dma((3,)),
-            dma((3,)),
-            dma((NZ,)),
-            dma((2, NZ)),
-            dma((3, NZ)),
-            dma((2, NZ)),
-            dma((2, 3, NZ)),
-            dma((2, 3, NZ)),
-            dma((2, 4, NZ)),
-            dma((2, 4, NZ)),
+            dma((1,)),
+            dma((2,)),
+            dma((2, 4)),
+            dma((2,)),
+            dma((2, 4)),
+            dma((2, 4)),
+            dma((2,)),
         ],
         compiler_params=pltpu.CompilerParams(collective_id=0, has_side_effects=True),
     )(frame_len, window_back, level_weight, queries, keys, values)

time: 38.3 us -> 34.2 us (0.89)
  Pallas kernels: 37.3 us -> 33 us
    pallas_call x1, Pallas kernels: 37.3 us -> 33 us  [body(): pl.pallas_call(functools.partial(kernel, tok * space_count), out_shape=pl...]
where the time goes in v5:
time: 34.2 us; the launch traced here: 33.8 us
  Pallas kernels  33 us (96%)
  local copies, waits for them, and re-layouts  0.88 us (3%)
    pallas_call x1, Pallas kernels, body(): pl.pallas_call(functools.partial(kernel, tok * space_count), out_shape=pl...  33 us
    unnamed x1, local copies, waits for them, and re-layouts  0.88 us

profile of v5, /device:TPU:7, one launch (start us, length us, event | category | flops | bytes accessed | tf_op | source)
XLA Modules:
  0.0 33.8 jit_solution(8983870176019696908)
XLA Ops:
  0.0 33.0 %shard_map.64 = bf16[128,3072]{1,0:T(8,128)(2,1)S(1)} custom-call(s32[1,4]{1,0:T(1,128)} %flen_hbm.1, s32[1,4]{1,0:T(1,128)} %wback_hbm.1, f32[3,24,128]{2,1,0:T(8,128)} %lw_hbm.1, bf16[128,3072]{1,0:T(8,128)(2,1)} %q_hbm.1, bf16[128,3072]{1,0:T(8,128)(2,1)} %k_hbm.1, bf16[128,3072]{1,0:T(8,128)(2,1)} %v_hbm.1), custom_call_target="tpu_custom_call" | custom-call | tf_op jit(solution)/shard_map/pallas_call | solution.py:571
  33.0 0.9 %copy.8 = bf16[128,3072]{1,0:T(8,128)(2,1)} copy(bf16[128,3072]{1,0:T(8,128)(2,1)S(1)} %shard_map.64) | data formatting | bytes 1572864

commit v6 on v5

v6 whole, which is shorter than its diff:
```python
import contextlib
import functools
import math

import jax
import jax.numpy as jnp
from jax import lax
from jax.experimental import pallas as pl
from jax.experimental.pallas import tpu as pltpu
from jax.sharding import PartitionSpec as P

MESH = pl.DeviceIdType.MESH
HEADS = 24
HALF = 12
D = 128
EPS = 1e-06
NY = 4
NZ = 8
CH = 3
SR = D // NZ
FIRST_Y = 0
FIRST_Z = (1, 2)
DELIVER = (0, 4, 1, 3, 5, 7, 2, 6)
GROUPS = ((0, 1, 7), (2, 6), (3, 5, 4))
GROUP = (0, 0, 1, 2, 2, 2, 1, 0)


def scope(name):
    return contextlib.nullcontext()


def kernel(
    block_tokens,
    flen_hbm,
    wback_hbm,
    lw_hbm,
    q_hbm,
    k_hbm,
    v_hbm,
    out,
    flen,
    wback,
    lw,
    q,
    k,
    v,
    bias,
    wrows,
    wt,
    loc,
    qs,
    part,
    sib_out,
    sib_in,
    y_out,
    y_in,
    z_out,
    z_in,
    x_out,
    lev,
    load_sem,
    misc_sem,
    step_sem,
    sent,
    sib_r,
    y_r,
    z_r,
    gz_r,
    gb_r,
    gy_r,
    zb_r,
    gs_r,
):
    f = lax.axis_index("frame")
    s = lax.axis_index("space")
    c = lax.rem(s, 2)
    y = lax.rem(s // 2, NY)
    z = s // (2 * NY)
    right = lax.rem(y + 1, NY)
    left = lax.rem(y + NY - 1, NY)
    opp = lax.rem(y + 2, NY)

    def at(zz, yy, cc):
        return (zz * NY + yy) * 2 + cc

    sib = (f, at(z, y, 1 - c))
    to_right = (f, at(z, right, c))
    to_left = (f, at(z, left, c))
    to_opp = (f, at(z, opp, c))
    across = ((to_opp, opp), (to_right, right), (to_left, left))
    chunk_at = (opp, right, left, y)

    def z_peer(step, ff=f):
        return (ff, at(lax.rem(z + step, NZ), y, c))

    def cols(head, count=1):
        return pl.ds(pl.multiple_of(head * D, D), count * D)

    def head_rows(yc, i):
        return pl.ds(pl.multiple_of((yc * CH + i) * D, D), D)

    def z_rows(zz):
        return pl.ds(pl.multiple_of(zz * SR, SR), SR)

    def send(src, dst, ssem, rsem, dev):
        return pltpu.make_async_remote_copy(
            src_ref=src, dst_ref=dst, send_sem=ssem, recv_sem=rsem, device_id=dev, device_id_type=MESH
        )

    def group(count, sem):
        whole = sib_in.at[pl.ds(0, count)]
        return send(whole, whole, sem, sem, sib)

    for i in range(CH):
        for half in range(2):
            for yc in chunk_at:
                span = cols((1 - c, c)[half] * HALF + yc * CH + i)
                for src, dst in ((k_hbm, k), (v_hbm, v)):
                    pltpu.make_async_copy(src.at[:, span], dst.at[:, span], load_sem.at[i, half]).start()

    def loaded(i, half):
        span = pl.ds(0, 2 * NY * D)
        pltpu.make_async_copy(k_hbm.at[:, span], k.at[:, span], load_sem.at[i, half]).wait()

    small = [
        pltpu.make_async_copy(src, dst, misc_sem.at[i])
        for i, (src, dst) in enumerate(((flen_hbm, flen), (wback_hbm, wback), (lw_hbm, lw), (q_hbm, q)))
    ]
    for cp in small:
        cp.start()

    barrier = pltpu.get_barrier_semaphore()
    z_next = (z_peer(1), z_peer(NZ - 1))
    x_next = ((lax.rem(f + 1, 4), s), (lax.rem(f + 3, 4), s))

    def signal(sem, devices):
        for dev in devices:
            pl.semaphore_signal(sem, inc=1, device_id=dev, device_id_type=MESH)

    def heard(i):
        with scope("h%d" % i):
            pl.semaphore_wait(step_sem.at[i], 2)

    signal(barrier, (sib, to_right, to_left, *z_next, *x_next))

    col = lax.broadcasted_iota(jnp.int32, (D, D), 1)

    def weight(index):
        return jnp.sum(jnp.where(col == index, wt[...], 0.0), -1, keepdims=True)

    def state(head):
        kk = k[:, cols(head)].astype(jnp.float32)
        kn = (kk * lax.rsqrt(jnp.mean(kk * kk, -1, keepdims=True) + EPS)).astype(jnp.bfloat16)
        return lax.dot_general(
            kn, v[:, cols(head)], (((0,), (0,)), ((), ())), preferred_element_type=jnp.float32
        )

    def attend(first, last):
        @pl.loop(first, last)
        def _(j):
            for i in range(CH):
                h = j * CH + i
                qq = q[:, cols(h)]
                scores = lax.dot_general(
                    qq, k[:, cols(h)], (((1,), (1,)), ((), ())), preferred_element_type=jnp.float32
                )
                scores = scores + bias[...]
                top = jnp.max(scores, -1, keepdims=True)
                p = jnp.exp((scores - top) * (1.0 / math.sqrt(D)))
                total = jnp.sum(p, -1, keepdims=True)
                mix = jnp.dot(p.astype(jnp.bfloat16), v[:, cols(h)], preferred_element_type=jnp.float32)
                loc[:, cols(h)] = mix * (weight(h) / total)
                q32 = qq.astype(jnp.float32)
                r = lax.rsqrt(jnp.mean(q32 * q32, -1, keepdims=True) + EPS)
                qs[0, :, cols(h)] = (q32 * (r * weight(HEADS + h))).astype(jnp.bfloat16)
                qs[1, :, cols(h)] = (q32 * (r * weight(2 * HEADS + h))).astype(jnp.bfloat16)

    sending = f < 3

    def states(i, half):
        with scope("st"):
            loaded(i, half)
            for yc in chunk_at:
                value = state((1 - c, c)[half] * HALF + yc * CH + i)
                if half == 0:
                    sib_out[head_rows(yc, i)] = value.astype(jnp.bfloat16)
                else:
                    part[head_rows(yc, i)] = value

    def send_sib(i):
        for yc in chunk_at:
            send(sib_out.at[head_rows(yc, i)], sib_in.at[head_rows(yc, i)], sent.at[0], sib_r.at[i], sib).start()

    def send_y(i):
        with scope("sw%d" % i):
            group(NY * D, sib_r.at[i]).wait_recv()
        for n, yc in enumerate(chunk_at):
            total = part[head_rows(yc, i)] + sib_in[head_rows(yc, i)].astype(jnp.float32)
            if n < 3:
                y_out[i, n] = total.astype(jnp.bfloat16)
                send(y_out.at[i, n], y_in.at[i, n], sent.at[1], y_r.at[i], across[n][0]).start()
            else:
                part[head_rows(yc, i)] = total

    summing = c == f
    slot = jnp.where(f == 2, 0, f)
    keeps = (f == 2) | summing

    def send_z(i):
        with scope("yw%d" % i):
            group(3 * D, y_r.at[i]).wait_recv()
        total = part[head_rows(y, i)]
        for n in range(3):
            total = total + y_in[i, n].astype(jnp.float32)
        part[head_rows(y, i)] = total
        z_out[i] = total.astype(jnp.bfloat16)

        def copy(step):
            zz = lax.rem(z + step, NZ)
            target = z_peer(step, jnp.where(f == 2, 2, c))
            return send(z_out.at[i, z_rows(zz)], z_in.at[slot, i, step], sent.at[2], z_r.at[slot, i], target)

        for step in (4, 3, 5, 2, 6, 1, 7):
            copy(step).start()

        @pl.when(jnp.logical_not(keeps))
        def _():
            copy(0).start()

    chunk = c * NY + y

    def deliver(i, step, kind, target, m):
        if i == FIRST_Y:
            dev, sem = (target, at(z, lax.rem(y + step, NY), c)), gb_r.at[m]
        else:
            dev, sem = z_peer(step, target), gz_r.at[m, FIRST_Z.index(i), GROUP[step]]
        send(x_out.at[kind, i], lev.at[m, chunk, i, z_rows(z)], sent.at[2 + target], sem, dev).start()

    def finish(i):
        @pl.when(keeps)
        def _():
            total = part[pl.ds(pl.multiple_of((y * CH + i) * D + z * SR, SR), SR)]
            with scope("zw%d" % i):
                group((NZ - 1) * SR, z_r.at[slot, i]).wait_recv()
            for step in range(1, NZ):
                total = total + z_in[slot, i, step].astype(jnp.float32)

            @pl.when(f == 2)
            def _():
                x_out[0, i] = total.astype(jnp.bfloat16)

            @pl.when(f < 2)
            def _():
                more = jnp.zeros_like(total)
                with scope("zc%d" % i):
                    group(NZ * SR, z_r.at[1 - slot, i]).wait_recv()
                for step in range(NZ):
                    more = more + z_in[1 - slot, i, step].astype(jnp.float32)
                x_out[1, i] = (total + more).astype(jnp.bfloat16)
                x_out[0, i] = jnp.where(f == 0, total, more).astype(jnp.bfloat16)

        steps = (2, 1, 3, 0) if i == FIRST_Y else DELIVER
        for who, pairs, first in (
            ((f == 0) & summing, ((1, 3, 1), (1, 2, 0), (0, 1, 0)), 0),
            ((f == 1) & summing, ((1, 3, 1), (1, 2, 0)), 0),
            ((f == 1) & summing, ((0, 1, 0),), 1),
            (f == 2, ((0, 3, 0),), 0),
        ):

            @pl.when(who)
            def _():
                for step in steps:
                    for pair in pairs:
                        if step >= first:
                            deliver(i, step, *pair)

        @pl.when((f == 1) & summing)
        def _():
            lev[0, chunk, i, z_rows(z)] = x_out[0, i]

    @pl.when(sending)
    def _():
        states(0, 0)
        states(0, 1)

    with scope("barrier"):
        pl.semaphore_wait(barrier, 7)
    signal(step_sem.at[0], z_next)
    signal(step_sem.at[3], (to_right, to_left))

    @pl.when(sending)
    def _():
        send_sib(0)
        states(1, 0)
        send_sib(1)
        states(1, 1)

    heard(0)
    signal(step_sem.at[1], z_next)
    heard(3)

    @pl.when(sending)
    def _():
        send_y(0)
        states(2, 0)
        send_sib(2)
        states(2, 1)

    heard(1)
    signal(step_sem.at[2], z_next)

    @pl.when(sending)
    def _():
        send_y(1)
        send_y(2)

    heard(2)
    signal(step_sem.at[4], z_next)

    @pl.when(jnp.logical_not(sending))
    def _():
        for i in range(CH):
            for half in range(2):
                loaded(i, half)

    for cp in small:
        cp.wait()
    row = lax.broadcasted_iota(jnp.int32, (D, D), 0)
    floor = jnp.full((D, D), 0, jnp.int32)
    start = 0
    for i in range(4):
        low = jnp.maximum(start - wback[0, i], 0)
        floor = jnp.where(row >= start, low, floor)
        start = start + flen[0, i]
    bias[...] = jnp.where((col <= row) & (col >= floor), 0.0, -jnp.inf)
    scale1 = 1.0 / math.sqrt(D * block_tokens)
    scale2 = 1.0 / math.sqrt(D * 2 * block_tokens)
    wrows[...] = jnp.zeros_like(wrows)
    wrows[0:HEADS] = lw[0]
    wrows[HEADS : 2 * HEADS] = jnp.where(f == 2, lw[2] * scale2, lw[1] * scale1)
    wrows[2 * HEADS : 3 * HEADS] = lw[2] * scale2
    wt[...] = jnp.transpose(wrows[...])

    with scope("att"):
        attend(0, 1)
    heard(4)
    for i, (first, last) in enumerate(((1, 2), (2, 3), (3, 5))):

        @pl.when(sending)
        def _():
            send_z(i)

        if i == 0:
            signal(step_sem.at[5], x_next)
        with scope("att"):
            attend(first, last)
    heard(5)
    for i, (first, last) in enumerate(((5, 6), (6, 7), (7, 8))):
        finish(i)
        with scope("att"):
            attend(first, last)

    def gather(n):
        def same(ref, ssem, rsem, dev):
            return send(ref, ref, ssem, rsem, dev)

        def gy(m, i, side, step):
            ref = lev.at[m, chunk, i, z_rows(lax.rem(z + NZ - step, NZ))]
            return same(ref, sent.at[6 + m], gy_r.at[m, FIRST_Z.index(i)], across[side][0])

        def gzb(m, step):
            ref = lev.at[m, pl.ds(c * NY, NY), FIRST_Y, z_rows(z)]
            return same(ref, sent.at[6 + m], zb_r.at[m], z_peer(step))

        def share(ref, m, i):
            same(ref, sent.at[8 + m], gs_r.at[m, i], sib).start()

        def read(m, i, half):
            for yc in (y, opp, left, right):
                index = half * NY + yc
                h = index * CH + i
                value = loc[:, cols(h)] + jnp.dot(
                    qs[m, :, cols(h)], lev[m, index, i], preferred_element_type=jnp.float32
                )
                if m == n - 1:
                    out[:, cols(h)] = value.astype(jnp.bfloat16)
                else:
                    loc[:, cols(h)] = value

        def unless_kept(count, less, sem):
            if n == 2:
                group(count, sem).wait_recv()
            else:
                kept = (f == 1) & summing

                @pl.when(kept)
                def _():
                    group(count - less, sem).wait_recv()

                @pl.when(jnp.logical_not(kept))
                def _():
                    group(count, sem).wait_recv()

        def forward(m, i, g):
            count, sem = SR * len(GROUPS[g]), gz_r.at[m, FIRST_Z.index(i), g]
            with scope("gz%d%d%d" % (m, i, g)):
                if g:
                    group(count, sem).wait_recv()
                else:
                    unless_kept(count, SR, sem)
            for step in GROUPS[g]:
                for side in range(3):
                    gy(m, i, side, step).start()
            if g == 2:
                share(lev.at[m, chunk, i], m, i)

        def forward_b(m):
            with scope("gb%d" % m):
                unless_kept(NY * SR, SR, gb_r.at[m])
            for step in (4, 3, 5, 2, 6, 1, 7):
                gzb(m, step).start()

        def pass_on(m, i):
            with scope("gy%d%d" % (m, i)):
                group(3 * D, gy_r.at[m, FIRST_Z.index(i)]).wait_recv()
            for yc in (opp, left, right):
                share(lev.at[m, c * NY + yc, i], m, i)

        def pass_on_b(m):
            with scope("zb%d" % m):
                group((NZ - 1) * NY * SR, zb_r.at[m]).wait_recv()
            share(lev.at[m, pl.ds(c * NY, NY), FIRST_Y], m, FIRST_Y)

        one, two = FIRST_Z
        if n == 1:
            forward_b(0)
            for i, g in ((one, 0), (one, 1), (two, 0), (one, 2), (two, 1), (two, 2)):
                forward(0, i, g)
        else:
            forward_b(0)
            forward(0, one, 0)
            forward(0, one, 1)
            forward_b(1)
            for m, i, g in (
                (0, one, 2),
                (1, one, 0),
                (0, two, 0),
                (1, one, 1),
                (0, two, 1),
                (1, one, 2),
                (0, two, 2),
                (1, two, 0),
                (1, two, 1),
                (1, two, 2),
            ):
                forward(m, i, g)
        for i in (FIRST_Y, one, two):
            for m in range(n):
                if i == FIRST_Y:
                    pass_on_b(m)
                else:
                    pass_on(m, i)
                read(m, i, c)
        for i in (FIRST_Y, one, two):
            for m in range(n):
                with scope("gs%d%d" % (m, i)):
                    group(NY * D, gs_r.at[m, i]).wait_recv()
                read(m, i, 1 - c)
        for m in range(n):
            group(3 * 2 * NZ * SR + (NZ - 1) * NY * SR, sent.at[6 + m]).wait_send()
            group(HALF * D, sent.at[8 + m]).wait_send()

    @pl.when(f == 0)
    def _():
        @pl.loop(0, 2 * NY)
        def _(j):
            out[:, cols(j * CH, CH)] = loc[:, cols(j * CH, CH)].astype(jnp.bfloat16)

    @pl.when((f == 1) | (f == 2))
    def _():
        gather(1)

    @pl.when(f == 3)
    def _():
        gather(2)

    @pl.when(sending)
    def _():
        with scope("tail"):
            group(HALF * D, sent.at[0]).wait_send()
        group(3 * CH * D, sent.at[1]).wait_send()

        @pl.when(keeps)
        def _():
            group(CH * (NZ - 1) * SR, sent.at[2]).wait_send()

        @pl.when(jnp.logical_not(keeps))
        def _():
            group(CH * NZ * SR, sent.at[2]).wait_send()

    everywhere = 2 * NZ * SR + NY * SR
    for who, target, count in (
        ((f < 2) & summing, 2, everywhere),
        ((f < 2) & summing, 3, everywhere),
        ((f == 0) & summing, 1, everywhere),
        ((f == 1) & summing, 1, everywhere - CH * SR),
        (f == 2, 3, everywhere),
    ):

        @pl.when(who)
        def _():
            group(count, sent.at[2 + target]).wait_send()


def body(space_count, queries, keys, values, level_weight, frame_len, window_back):
    tok, width = queries.shape
    f32, bf16 = jnp.float32, jnp.bfloat16
    dma = pltpu.SemaphoreType.DMA
    anyspec = pl.BlockSpec(memory_space=pl.ANY)
    return pl.pallas_call(
        functools.partial(kernel, tok * space_count),
        out_shape=pltpu.VMEM((tok, width), bf16),
        in_specs=[anyspec] * 6,
        out_specs=pl.BlockSpec(memory_space=pltpu.VMEM),
        scratch_shapes=[
            pltpu.SMEM((1, 4), jnp.int32),
            pltpu.SMEM((1, 4), jnp.int32),
            pltpu.VMEM(level_weight.shape, f32),
            pltpu.VMEM((tok, width), bf16),
            pltpu.VMEM((tok, width), bf16),
            pltpu.VMEM((tok, width), bf16),
            pltpu.VMEM((D, D), f32),
            pltpu.VMEM((D, D), f32),
            pltpu.VMEM((D, D), f32),
            pltpu.VMEM((tok, width), f32),
            pltpu.VMEM((2, tok, width), bf16),
            pltpu.VMEM((HALF * D, D), f32),
            pltpu.VMEM((HALF * D, D), bf16),
            pltpu.VMEM((HALF * D, D), bf16),
            pltpu.VMEM((CH, 3, D, D), bf16),
            pltpu.VMEM((CH, 3, D, D), bf16),
            pltpu.VMEM((CH, D, D), bf16),
            pltpu.VMEM((2, CH, NZ, SR, D), bf16),
            pltpu.VMEM((2, CH, SR, D), bf16),
            pltpu.VMEM((2, 2 * NY, CH, D, D), bf16),
            dma((CH, 2)),
            dma((4,)),
            pltpu.SemaphoreType.REGULAR((6,)),
            dma((10,)),
            dma((CH,)),
            dma((CH,)),
            dma((2, CH)),
            dma((2, 2, 3)),
            dma((2,)),
            dma((2, 2)),
            dma((2,)),
            dma((2, CH)),
        ],
        compiler_params=pltpu.CompilerParams(collective_id=0, has_side_effects=True),
    )(frame_len, window_back, level_weight, queries, keys, values)


def solution(mesh):
    return jax.shard_map(
        functools.partial(body, mesh.shape["space"]),
        mesh=mesh,
        in_specs=(
            P(("frame", "space"), None),
            P(("frame", "space"), None),
            P(("frame", "space"), None),
            P(None, None, ("frame", "space")),
            P(("frame", "space"), None),
            P(("frame", "space"), None),
        ),
        out_specs=P(("frame", "space"), None),
        check_vma=False,
    )
```

time: 34.2 us -> 33.2 us (0.971)
  Pallas kernels: 33 us -> 32.2 us
    pallas_call x1, Pallas kernels: 33 us -> 32.2 us  [body(): pl.pallas_call(functools.partial(kernel, tok * space_count), out_shape=pl...]
where the time goes in v6:
time: 33.2 us; the launch traced here: 33.1 us
  Pallas kernels  32.2 us (97%)
  local copies, waits for them, and re-layouts  0.88 us (3%)
    pallas_call x1, Pallas kernels, body(): pl.pallas_call(functools.partial(kernel, tok * space_count), out_shape=pl...  32.2 us
    unnamed x1, local copies, waits for them, and re-layouts  0.88 us

profile of v6, /device:TPU:7, one launch (start us, length us, event | category | flops | bytes accessed | tf_op | source)
XLA Modules:
  0.0 33.1 jit_solution(3458223735455390627)
XLA Ops:
  0.0 32.2 %shard_map.64 = bf16[128,3072]{1,0:T(8,128)(2,1)S(1)} custom-call(s32[1,4]{1,0:T(1,128)} %flen_hbm.1, s32[1,4]{1,0:T(1,128)} %wback_hbm.1, f32[3,24,128]{2,1,0:T(8,128)} %lw_hbm.1, bf16[128,3072]{1,0:T(8,128)(2,1)} %q_hbm.1, bf16[128,3072]{1,0:T(8,128)(2,1)} %k_hbm.1, bf16[128,3072]{1,0:T(8,128)(2,1)} %v_hbm.1), custom_call_target="tpu_custom_call" | custom-call | tf_op jit(solution)/shard_map/pallas_call | solution.py:520
  32.2 0.9 %copy.8 = bf16[128,3072]{1,0:T(8,128)(2,1)} copy(bf16[128,3072]{1,0:T(8,128)(2,1)S(1)} %shard_map.64) | data formatting | bytes 1572864

commit v7 on v6

--- a/solution.py
+++ b/solution.py
@@ -131,17 +131,18 @@
 
     barrier = pltpu.get_barrier_semaphore()
     z_next = (z_peer(1), z_peer(NZ - 1))
+    z_second = (z_peer(2), z_peer(NZ - 2))
     x_next = ((lax.rem(f + 1, 4), s), (lax.rem(f + 3, 4), s))
 
     def signal(sem, devices):
         for dev in devices:
             pl.semaphore_signal(sem, inc=1, device_id=dev, device_id_type=MESH)
 
-    def heard(i):
+    def heard(i, count=2):
         with scope("h%d" % i):
-            pl.semaphore_wait(step_sem.at[i], 2)
-
-    signal(barrier, (sib, to_right, to_left, *z_next, *x_next))
+            pl.semaphore_wait(step_sem.at[i], count)
+
+    signal(barrier, (sib, to_right, to_left, to_opp, *z_next, *x_next, *z_second))
 
     col = lax.broadcasted_iota(jnp.int32, (D, D), 1)
 
@@ -284,38 +285,33 @@
         states(0, 1)
 
     with scope("barrier"):
-        pl.semaphore_wait(barrier, 7)
-    signal(step_sem.at[0], z_next)
-    signal(step_sem.at[3], (to_right, to_left))
+        pl.semaphore_wait(barrier, 10)
+    signal(step_sem.at[0], z_second)
 
     @pl.when(sending)
     def _():
         send_sib(0)
         states(1, 0)
         send_sib(1)
-        states(1, 1)
-
-    heard(0)
-    signal(step_sem.at[1], z_next)
-    heard(3)
-
-    @pl.when(sending)
-    def _():
-        send_y(0)
         states(2, 0)
         send_sib(2)
+
+    @pl.when(sending)
+    def _():
+        send_y(0)
+        states(1, 1)
+
+    @pl.when(sending)
+    def _():
+        send_y(1)
         states(2, 1)
 
-    heard(1)
-    signal(step_sem.at[2], z_next)
+    heard(0)
+    signal(step_sem.at[1], (*z_next, *z_second))
 
     @pl.when(sending)
     def _():
-        send_y(1)
         send_y(2)
-
-    heard(2)
-    signal(step_sem.at[4], z_next)
 
     @pl.when(jnp.logical_not(sending))
     def _():
@@ -342,23 +338,23 @@
     wt[...] = jnp.transpose(wrows[...])
 
     with scope("att"):
-        attend(0, 1)
-    heard(4)
-    for i, (first, last) in enumerate(((1, 2), (2, 3), (3, 5))):
+        attend(0, 2)
+    heard(1, 4)
+    for i, (first, last) in enumerate(((2, 3), (3, 4), (4, 6))):
 
         @pl.when(sending)
         def _():
             send_z(i)
 
         if i == 0:
-            signal(step_sem.at[5], x_next)
+            signal(step_sem.at[2], x_next)
         with scope("att"):
             attend(first, last)
-    heard(5)
-    for i, (first, last) in enumerate(((5, 6), (6, 7), (7, 8))):
+    heard(2)
+    for i in range(CH):
         finish(i)
-        with scope("att"):
-            attend(first, last)
+    with scope("att"):
+        attend(6, 8)
 
     def gather(n):
         def same(ref, ssem, rsem, dev):
@@ -375,17 +371,22 @@
         def share(ref, m, i):
             same(ref, sent.at[8 + m], gs_r.at[m, i], sib).start()
 
-        def read(m, i, half):
+        def read(i, half):
             for yc in (y, opp, left, right):
                 index = half * NY + yc
                 h = index * CH + i
-                value = loc[:, cols(h)] + jnp.dot(
-                    qs[m, :, cols(h)], lev[m, index, i], preferred_element_type=jnp.float32
-                )
-                if m == n - 1:
-                    out[:, cols(h)] = value.astype(jnp.bfloat16)
-                else:
-                    loc[:, cols(h)] = value
+                value = loc[:, cols(h)]
+                for m in range(n):
+                    value = value + jnp.dot(
+                        qs[m, :, cols(h)], lev[m, index, i], preferred_element_type=jnp.float32
+                    )
+                out[:, cols(h)] = value.astype(jnp.bfloat16)
+
+        def read_shared(i):
+            for m in range(n):
+                with scope("gs%d%d" % (m, i)):
+                    group(NY * D, gs_r.at[m, i]).wait_recv()
+            read(i, 1 - c)
 
         def unless_kept(count, less, sem):
             if n == 2:
@@ -439,9 +440,9 @@
         else:
             forward_b(0)
             forward(0, one, 0)
-            forward(0, one, 1)
             forward_b(1)
             for m, i, g in (
+                (0, one, 1),
                 (0, one, 2),
                 (1, one, 0),
                 (0, two, 0),
@@ -454,18 +455,19 @@
                 (1, two, 2),
             ):
                 forward(m, i, g)
+        pass_on_b(0)
+        if n == 2:
+            pass_on(0, one)
+            pass_on_b(1)
+        read(FIRST_Y, c)
+        pass_on(n - 1, one)
+        read(one, c)
+        if n == 2:
+            pass_on(0, two)
+        pass_on(n - 1, two)
+        read(two, c)
         for i in (FIRST_Y, one, two):
-            for m in range(n):
-                if i == FIRST_Y:
-                    pass_on_b(m)
-                else:
-                    pass_on(m, i)
-                read(m, i, c)
-        for i in (FIRST_Y, one, two):
-            for m in range(n):
-                with scope("gs%d%d" % (m, i)):
-                    group(NY * D, gs_r.at[m, i]).wait_recv()
-                read(m, i, 1 - c)
+            read_shared(i)
         for m in range(n):
             group(3 * 2 * NZ * SR + (NZ - 1) * NY * SR, sent.at[6 + m]).wait_send()
             group(HALF * D, sent.at[8 + m]).wait_send()
@@ -545,7 +547,7 @@
             pltpu.VMEM((2, 2 * NY, CH, D, D), bf16),
             dma((CH, 2)),
             dma((4,)),
-            pltpu.SemaphoreType.REGULAR((6,)),
+            pltpu.SemaphoreType.REGULAR((3,)),
             dma((10,)),
             dma((CH,)),
             dma((CH,)),

time: 33.2 us -> 33 us (level)
  no operation moved by 1% of the time
where the time goes in v7:
time: 33 us; the launch traced here: 32.9 us
  Pallas kernels  32 us (97%)
  local copies, waits for them, and re-layouts  0.88 us (3%)
    pallas_call x1, Pallas kernels, body(): pl.pallas_call(functools.partial(kernel, tok * space_count), out_shape=pl...  32 us
    unnamed x1, local copies, waits for them, and re-layouts  0.88 us

profile of v7, /device:TPU:7, one launch (start us, length us, event | category | flops | bytes accessed | tf_op | source)
XLA Modules:
  0.0 32.9 jit_solution(11807340970835086477)
XLA Ops:
  0.0 32.0 %shard_map.64 = bf16[128,3072]{1,0:T(8,128)(2,1)S(1)} custom-call(s32[1,4]{1,0:T(1,128)} %flen_hbm.1, s32[1,4]{1,0:T(1,128)} %wback_hbm.1, f32[3,24,128]{2,1,0:T(8,128)} %lw_hbm.1, bf16[128,3072]{1,0:T(8,128)(2,1)} %q_hbm.1, bf16[128,3072]{1,0:T(8,128)(2,1)} %k_hbm.1, bf16[128,3072]{1,0:T(8,128)(2,1)} %v_hbm.1), custom_call_target="tpu_custom_call" | custom-call | tf_op jit(solution)/shard_map/pallas_call | solution.py:522
  32.0 0.9 %copy.8 = bf16[128,3072]{1,0:T(8,128)(2,1)} copy(bf16[128,3072]{1,0:T(8,128)(2,1)S(1)} %shard_map.64) | data formatting | bytes 1572864

commit v8 on v7

--- a/solution.py
+++ b/solution.py
@@ -87,8 +87,8 @@
     to_right = (f, at(z, right, c))
     to_left = (f, at(z, left, c))
     to_opp = (f, at(z, opp, c))
-    across = ((to_opp, opp), (to_right, right), (to_left, left))
-    chunk_at = (opp, right, left, y)
+    across = ((to_right, right), (to_left, left), (to_opp, opp))
+    chunk_at = (right, left, opp, y)
 
     def z_peer(step, ff=f):
         return (ff, at(lax.rem(z + step, NZ), y, c))

time: 33 us -> 32.8 us (level)
  no operation moved by 1% of the time
where the time goes in v8:
time: 32.8 us; the launch traced here: 32.7 us
  Pallas kernels  31.8 us (97%)
  local copies, waits for them, and re-layouts  0.88 us (3%)
    pallas_call x1, Pallas kernels, body(): pl.pallas_call(functools.partial(kernel, tok * space_count), out_shape=pl...  31.8 us
    unnamed x1, local copies, waits for them, and re-layouts  0.88 us

profile of v8, /device:TPU:7, one launch (start us, length us, event | category | flops | bytes accessed | tf_op | source)
XLA Modules:
  0.0 32.7 jit_solution(13989537230572042144)
XLA Ops:
  0.0 31.8 %shard_map.64 = bf16[128,3072]{1,0:T(8,128)(2,1)S(1)} custom-call(s32[1,4]{1,0:T(1,128)} %flen_hbm.1, s32[1,4]{1,0:T(1,128)} %wback_hbm.1, f32[3,24,128]{2,1,0:T(8,128)} %lw_hbm.1, bf16[128,3072]{1,0:T(8,128)(2,1)} %q_hbm.1, bf16[128,3072]{1,0:T(8,128)(2,1)} %k_hbm.1, bf16[128,3072]{1,0:T(8,128)(2,1)} %v_hbm.1), custom_call_target="tpu_custom_call" | custom-call | tf_op jit(solution)/shard_map/pallas_call | solution.py:522
  31.8 0.9 %copy.8 = bf16[128,3072]{1,0:T(8,128)(2,1)} copy(bf16[128,3072]{1,0:T(8,128)(2,1)S(1)} %shard_map.64) | data formatting | bytes 1572864

commit v9 on v8

--- a/solution.py
+++ b/solution.py
@@ -235,7 +235,7 @@
             dev, sem = (target, at(z, lax.rem(y + step, NY), c)), gb_r.at[m]
         else:
             dev, sem = z_peer(step, target), gz_r.at[m, FIRST_Z.index(i), GROUP[step]]
-        send(x_out.at[kind, i], lev.at[m, chunk, i, z_rows(z)], sent.at[2 + target], sem, dev).start()
+        send(x_out.at[kind, i], lev.at[m, chunk, i, z_rows(z)], sent.at[2], sem, dev).start()
 
     def finish(i):
         @pl.when(keeps)
@@ -340,7 +340,7 @@
     with scope("att"):
         attend(0, 2)
     heard(1, 4)
-    for i, (first, last) in enumerate(((2, 3), (3, 4), (4, 6))):
+    for i, (first, last) in enumerate(((2, 3), (3, 4), (4, 5))):
 
         @pl.when(sending)
         def _():
@@ -354,7 +354,7 @@
     for i in range(CH):
         finish(i)
     with scope("att"):
-        attend(6, 8)
+        attend(5, 8)
 
     def gather(n):
         def same(ref, ssem, rsem, dev):
@@ -362,14 +362,14 @@
 
         def gy(m, i, side, step):
             ref = lev.at[m, chunk, i, z_rows(lax.rem(z + NZ - step, NZ))]
-            return same(ref, sent.at[6 + m], gy_r.at[m, FIRST_Z.index(i)], across[side][0])
+            return same(ref, sent.at[3 + m], gy_r.at[m, FIRST_Z.index(i)], across[side][0])
 
         def gzb(m, step):
             ref = lev.at[m, pl.ds(c * NY, NY), FIRST_Y, z_rows(z)]
-            return same(ref, sent.at[6 + m], zb_r.at[m], z_peer(step))
+            return same(ref, sent.at[3 + m], zb_r.at[m], z_peer(step))
 
         def share(ref, m, i):
-            same(ref, sent.at[8 + m], gs_r.at[m, i], sib).start()
+            same(ref, sent.at[5 + m], gs_r.at[m, i], sib).start()
 
         def read(i, half):
             for yc in (y, opp, left, right):
@@ -469,8 +469,8 @@
         for i in (FIRST_Y, one, two):
             read_shared(i)
         for m in range(n):
-            group(3 * 2 * NZ * SR + (NZ - 1) * NY * SR, sent.at[6 + m]).wait_send()
-            group(HALF * D, sent.at[8 + m]).wait_send()
+            group(3 * 2 * NZ * SR + (NZ - 1) * NY * SR, sent.at[3 + m]).wait_send()
+            group(HALF * D, sent.at[5 + m]).wait_send()
 
     @pl.when(f == 0)
     def _():
@@ -492,26 +492,17 @@
             group(HALF * D, sent.at[0]).wait_send()
         group(3 * CH * D, sent.at[1]).wait_send()
 
-        @pl.when(keeps)
-        def _():
-            group(CH * (NZ - 1) * SR, sent.at[2]).wait_send()
-
-        @pl.when(jnp.logical_not(keeps))
-        def _():
-            group(CH * NZ * SR, sent.at[2]).wait_send()
-
-    everywhere = 2 * NZ * SR + NY * SR
-    for who, target, count in (
-        ((f < 2) & summing, 2, everywhere),
-        ((f < 2) & summing, 3, everywhere),
-        ((f == 0) & summing, 1, everywhere),
-        ((f == 1) & summing, 1, everywhere - CH * SR),
-        (f == 2, 3, everywhere),
+    own, everywhere = CH * (NZ - 1) * SR, 2 * NZ * SR + NY * SR
+    for who, count in (
+        ((f < 3) & jnp.logical_not(keeps), CH * NZ * SR),
+        ((f == 0) & summing, own + 3 * everywhere),
+        ((f == 1) & summing, own + 3 * everywhere - CH * SR),
+        (f == 2, own + everywhere),
     ):
 
         @pl.when(who)
         def _():
-            group(count, sent.at[2 + target]).wait_send()
+            group(count, sent.at[2]).wait_send()
 
 
 def body(space_count, queries, keys, values, level_weight, frame_len, window_back):
@@ -548,7 +539,7 @@
             dma((CH, 2)),
             dma((4,)),
             pltpu.SemaphoreType.REGULAR((3,)),
-            dma((10,)),
+            dma((7,)),
             dma((CH,)),
             dma((CH,)),
             dma((2, CH)),

time: 32.8 us -> 32.6 us (level)
  no operation moved by 1% of the time
where the time goes in v9:
time: 32.6 us; the launch traced here: 32.5 us
  Pallas kernels  31.6 us (97%)
  local copies, waits for them, and re-layouts  0.88 us (3%)
    pallas_call x1, Pallas kernels, body(): pl.pallas_call(functools.partial(kernel, tok * space_count), out_shape=pl...  31.6 us
    unnamed x1, local copies, waits for them, and re-layouts  0.88 us

profile of v9, /device:TPU:7, one launch (start us, length us, event | category | flops | bytes accessed | tf_op | source)
XLA Modules:
  0.0 32.5 jit_solution(15151077610746266076)
XLA Ops:
  0.0 31.6 %shard_map.64 = bf16[128,3072]{1,0:T(8,128)(2,1)S(1)} custom-call(s32[1,4]{1,0:T(1,128)} %flen_hbm.1, s32[1,4]{1,0:T(1,128)} %wback_hbm.1, f32[3,24,128]{2,1,0:T(8,128)} %lw_hbm.1, bf16[128,3072]{1,0:T(8,128)(2,1)} %q_hbm.1, bf16[128,3072]{1,0:T(8,128)(2,1)} %k_hbm.1, bf16[128,3072]{1,0:T(8,128)(2,1)} %v_hbm.1), custom_call_target="tpu_custom_call" | custom-call | tf_op jit(solution)/shard_map/pallas_call | solution.py:513
  31.6 0.9 %copy.8 = bf16[128,3072]{1,0:T(8,128)(2,1)} copy(bf16[128,3072]{1,0:T(8,128)(2,1)S(1)} %shard_map.64) | data formatting | bytes 1572864
